TPU v7x, 128 devices: a whole 4x4x4 slice. The times are simulated.
128 devices in a mesh: row: 8 (over x, y_lo), col: 8 (over z, y_hi), depth: 2 (over core).
Axes of the slice: x: 4, y: 4 (y_hi: 2, y_lo: 2; y = y_hi * 2 + y_lo), z: 4, core: 2. Of those that a mesh axis runs over, the one named last changes fastest.
Arguments:
- amplitudes: bfloat16 [20480, 20480], P('row', 'col'), may hold values from -0.109375 to 0.109375
- coulomb_vertex: bfloat16 [256, 20480], P('depth', ('row', 'col')), may hold values from -1.5 to 1.5
Outputs:
- cycle_residual: bfloat16 [20480, 20480], P('row', ('col', 'depth'))
- structure_factor: float32 [256], P('depth')
All inputs are finite; a program needn't handle non-finite values.
Results may differ from a plain program's by a relative error of at most 0.0057.
Values may be sent and summed in bfloat16 or wider, within the bound.
No kernel may reach another device: no remote copies, remote signals or barrier semaphores. Data moves between devices by JAX's collectives and lax.ppermute only.
A program may use at most 128 MiB of HBM per device.

v0:
```python
import jax
import jax.numpy as jnp
from jax import lax
from jax.sharding import PartitionSpec as P


def broadcast(array, axis, root):
    mine = lax.axis_index(axis) == root
    return lax.psum(jnp.where(mine, array, jnp.zeros_like(array)), axis)


def body(amplitudes, coulomb_vertex):
    row_index = lax.axis_index("row")
    col_index = lax.axis_index("col")
    block_width = amplitudes.shape[0]
    on_diagonal = (row_index == col_index).astype(jnp.float32)
    vertex_rows = lax.all_gather(coulomb_vertex, "col", axis=1, tiled=True)
    vertex_cols = broadcast(vertex_rows, "row", col_index)
    dressing = jnp.dot(vertex_rows, amplitudes, preferred_element_type=jnp.float32)
    factor_part = jnp.sum(dressing * vertex_cols.astype(jnp.float32), axis=1)
    structure_factor = lax.psum(factor_part, ("row", "col"))
    dressed_term = dressing + on_diagonal * vertex_rows.astype(jnp.float32)
    dressed_part = lax.psum_scatter(dressed_term, "row", scatter_dimension=1, tiled=True)
    dressed = dressed_part.astype(jnp.bfloat16)
    everything = lax.all_gather(dressed, ("row", "col"), axis=1, tiled=True)
    fields_here = everything.shape[0]
    grid_side = lax.axis_size("row")
    ordered = everything.reshape(fields_here, grid_side, grid_side, dressed.shape[1])
    ordered = jnp.transpose(ordered, (0, 2, 1, 3)).reshape(
        fields_here, grid_side * grid_side * dressed.shape[1]
    )
    dressed_cols = lax.dynamic_slice_in_dim(ordered, col_index * block_width, block_width, 1)
    dressed_rows = lax.dynamic_slice_in_dim(ordered, row_index * block_width, block_width, 1)
    cols_all = lax.all_to_all(dressed_cols, "depth", split_axis=1, concat_axis=0, tiled=True)
    rows_all = lax.all_gather(dressed_rows, "depth", axis=0, tiled=True)
    product = lax.dot_general(
        rows_all, cols_all, (((0,), (0,)), ((), ())), preferred_element_type=jnp.float32
    )
    cycle_residual = product.astype(jnp.bfloat16)
    return (cycle_residual, structure_factor)


def solution(mesh):
    return jax.shard_map(
        body,
        mesh=mesh,
        in_specs=(P("row", "col"), P("depth", ("row", "col"))),
        out_specs=(P("row", ("col", "depth")), P("depth")),
        check_vma=False,
    )
```

profile of v0, /device:TPU:1, one launch (start us, length us, event | category | flops | bytes accessed | tf_op | source)
XLA Modules:
  0.0 711.8 jit_solution(17845553352122211983)
XLA Ops:
  7.2 0.0 all-reduce.2.cloned.1.call-start
  7.2 33.1 %all_gather.9 = bf16[128,2560]{0,1:T(8,128)(2,1)S(1)} all-gather(bf16[128,320]{0,1:T(8,128)(2,1)} %param.3), channel_id=1, replica_groups=mesh['row'=8,'col'=8,'depth'=2] {'col'}, dimensions={1}, use_global_device_ids=true | all-gather | bytes 737280 | tf_op jit(solution)/shard_map/all_gather | solution.py:17
  40.3 0.2 copy.17
  40.6 0.9 broadcast_select_fusion
  41.5 0.0 all-reduce.2.cloned.1.call-update
  41.5 0.0 reduce-scatter.4.cloned.1.call-start
  41.5 77.2 %all-reduce.2.cloned.1.call-done = bf16[128,2560]{1,0:T(8,128)(2,1)} async-done(((bf16[128,2560]{1,0:T(8,128)(2,1)}), bf16[128,2560]{1,0:T(8,128)(2,1)}) %all-reduce.2.cloned.1.call-update) | async-done | bytes 655376 | tf_op jit(solution)/shard_map/psum | solution.py:9
  118.7 6.9 multiply_reduce_fusion
  125.6 1.5 copy.22
  127.1 0.0 reduce-scatter.4.cloned.1.call-update
  127.1 0.0 all-gather.3.cloned.1.call-start
  127.1 42.3 %reduce-scatter.4.cloned.1.call-done = f32[320,128]{1,0:T(8,128)} async-done(((f32[2560,128]{1,0:T(8,128)}), f32[320,128]{1,0:T(8,128)}) %reduce-scatter.4.cloned.1.call-update) | async-done | bytes 163856
  169.5 1.6 bitcast_convert_fusion
  171.0 0.0 all-gather.3.cloned.1.call-update
  171.1 0.0 all-gather.5.cloned.1.call-start
  171.1 301.0 %all-gather.3.cloned.1.call-done = bf16[128,20480]{0,1:T(8,128)(2,1)} async-done(((bf16[128,320]{0,1:T(8,128)(2,1)}), bf16[128,20480]{0,1:T(8,128)(2,1)}) %all-gather.3.cloned.1.call-update) | async-done | bytes 5242896 | tf_op jit(solution)/shard_map/all_gather | solution.py:25
  472.2 2.9 copy.19
  475.1 0.9 constant_dynamic-slice_fusion
  476.0 0.0 all-gather.5.cloned.1.call-update
  476.1 148.3 %psum.15 = f32[128]{0:T(128)} all-reduce(f32[128]{0:T(128)S(1)} %get-tuple-element.4), channel_id=1, replica_groups=mesh['row'=8,'col'=8,'depth'=2] {'row','col'}, use_global_device_ids=true, to_apply=%region_3.4 | all-reduce | flops 128 | bytes 1024 | tf_op jit(solution)/shard_map/psum | solution.py:21
  624.3 74.7 %all_to_all.19 = bf16[128,2,1280]{0,2,1:T(8,128)(2,1)S(1)} all-to-all(bf16[128,2,1280]{0,2,1:T(8,128)(2,1)S(1)} %bitcast.19), channel_id=1, replica_groups=mesh['row'=8,'col'=8,'depth'=2] {'depth'}, dimensions={1} | all-to-all | bytes 1310720 | tf_op jit(solution)/shard_map/all_to_all | solution.py:34
  699.0 0.2 copy.20
  699.3 0.0 all-gather.5.cloned.1.call-done
  699.3 6.0 convolution_convert_fusion
Async XLA Ops:
  7.2 111.5 %all-reduce.2.cloned.1.call-start = ((), (), s32[]{:S(2)}) async-start(), calls=%async_computation.4 | async-start | bytes 1310720 | tf_op jit(solution)/shard_map/psum | solution.py:9
  41.5 128.0 %reduce-scatter.4.cloned.1.call-start = ((), (), s32[]{:S(2)}) async-start(), calls=%async_computation.5 | async-start | bytes 1474560
  127.1 345.1 %all-gather.3.cloned.1.call-start = ((), (), s32[]{:S(2)}) async-start(), calls=%async_computation.2 | async-start | bytes 5324800 | tf_op jit(solution)/shard_map/all_gather | solution.py:25
  171.1 528.3 %all-gather.5.cloned.1.call-start = ((), (), s32[]{:S(2)}) async-start(), calls=%async_computation.3 | async-start | bytes 1966080 | tf_op jit(solution)/shard_map/all_gather | solution.py:35
Sparse Core Ops, SparseCore 0:
  41.6 77.0 all-reduce.1
  127.2 42.2 reduce-scatter.3
  171.7 300.4 all-gather.2
  476.2 51.9 all-gather.4
where the time goes:
time: 712 us
  waiting for transfers between devices  421 us (59%)
  blocking collectives  256 us (36%)
  between operations  13.8 us (2%)
  matrix products  12.9 us (2%)
    all_gather x1, waiting for transfers between devices, body(): everything = lax.all_gather(dressed, ('row', 'col'), axis=1, tiled=True)  301 us
    psum x1, blocking collectives, body(): structure_factor = lax.psum(factor_part, ('row', 'col'))  148 us
    psum x1, waiting for transfers between devices, broadcast(): return lax.psum(jnp.where(mine, array, jnp.zeros_like(array)), axis)  77.2 us
    all_to_all x1, blocking collectives, body(): lax.all_to_all(dressed_cols, 'depth', split_axis=1, concat_axis=0, tiled=...  74.7 us
    unnamed x5, waiting for transfers between devices  42.4 us
    all_gather x1, blocking collectives, body(): vertex_rows = lax.all_gather(coulomb_vertex, 'col', axis=1, tiled=True)  33.1 us
  transfers between devices with their start and end apart: 4, of which 3 were waited for; matrix products, arithmetic and copies ran while one was open for 0% of the time, Pallas kernels for 0%

commit v1 on v0

v1 whole, which is shorter than its diff:
```python
import jax
import jax.numpy as jnp
from jax import lax
from jax.sharding import PartitionSpec as P

F32 = jnp.float32
BF16 = jnp.bfloat16


def split_three(x):
    parts = []
    for _ in range(3):
        head = lax.reduce_precision(x, 8, 7)
        parts.append(head.astype(BF16))
        x = x - head
    return jnp.stack(parts)


def gather_blocks(block, axis):
    copies = jnp.broadcast_to(block[None], (lax.axis_size(axis),) + block.shape)
    return lax.all_to_all(copies, axis, 0, 0)


def body(amplitudes, coulomb_vertex):
    rows = lax.axis_size("row")
    cols = lax.axis_size("col")
    fields, width = coulomb_vertex.shape
    depth_index = lax.axis_index("depth")
    across = [(r * cols + c, c * rows + r) for r in range(rows) for c in range(cols)]

    shard = coulomb_vertex.T
    shard_across = lax.ppermute(shard, ("row", "col"), across)
    vertex_rows = gather_blocks(shard, "col").reshape(-1, fields)
    partial = lax.dot_general(
        vertex_rows, amplitudes, (((0,), (0,)), ((), ())), preferred_element_type=F32
    )
    partial = partial.T.astype(BF16).reshape(rows, width, fields)
    partial = lax.all_to_all(partial, "row", 0, 0)
    dressing = jnp.sum(partial.astype(F32), axis=0)
    shard_across = shard_across.astype(F32)
    factor = jnp.sum(shard_across * dressing, axis=0)
    dressed = (shard_across + dressing).astype(BF16)

    pad = jnp.zeros((13, fields), BF16)
    block = jnp.concatenate([dressed, split_three(factor), pad])
    along = gather_blocks(block, "col")
    factor = jnp.sum(along[:, width : width + 3].astype(F32), axis=(0, 1))
    tail = jnp.concatenate([dressed, split_three(factor), pad])
    chunks = jnp.concatenate(
        [along[:, :width], jnp.broadcast_to(tail[None], (rows,) + tail.shape)], axis=1
    )
    arrived = lax.all_to_all(chunks, "row", 0, 0)
    structure_factor = jnp.sum(arrived[:, 2 * width : 2 * width + 3].astype(F32), axis=(0, 1))
    row_block = arrived[:, :width].reshape(-1, fields)
    col_block = arrived[:, width : 2 * width].reshape(-1, fields)

    half = col_block.shape[0] // 2
    swap = [(0, 1), (1, 0)]
    cols_mine = lax.dynamic_slice_in_dim(col_block, depth_index * half, half, 0)
    cols_send = lax.dynamic_slice_in_dim(col_block, (1 - depth_index) * half, half, 0)
    cols_other = lax.ppermute(cols_send, "depth", swap)
    rows_other = lax.ppermute(row_block, "depth", swap)
    left = jnp.concatenate([row_block, rows_other], axis=1)
    right = jnp.concatenate([cols_mine, cols_other], axis=1)
    product = lax.dot_general(
        left, right, (((1,), (1,)), ((), ())), preferred_element_type=F32
    )
    return (product.astype(BF16), structure_factor)


def solution(mesh):
    return jax.shard_map(
        body,
        mesh=mesh,
        in_specs=(P("row", "col"), P("depth", ("row", "col"))),
        out_specs=(P("row", ("col", "depth")), P("depth")),
        check_vma=False,
    )
```

time: 712 us -> 92.8 us (0.13)
  waiting for transfers between devices: 421 us -> 9.52 us
  blocking collectives: 256 us -> 57.1 us
  between operations: 13.8 us -> 0.72 us
  starting transfers between devices: 0.16 us -> 10.2 us
    all_gather x2 -> x0, waiting for transfers between devices: 301 us -> none  [the longest x1 301 us: body(): everything = lax.all_gather(dressed, ('row', 'col'), axis=1, tiled=True)]
    psum x1 -> x0, blocking collectives: 148 us -> none  [body(): structure_factor = lax.psum(factor_part, ('row', 'col'))]
    psum x1 -> x0, waiting for transfers between devices: 77.2 us -> none  [broadcast(): return lax.psum(jnp.where(mine, array, jnp.zeros_like(array)), axis)]
    unnamed x5 -> x0, waiting for transfers between devices: 42.4 us -> none
    all_gather x1 -> x0, blocking collectives: 33.1 us -> none  [body(): vertex_rows = lax.all_gather(coulomb_vertex, 'col', axis=1, tiled=True)]
    all_to_all x1 -> x3, blocking collectives: 74.7 us -> 57.1 us  [the longest x2 38.2 us: gather_blocks(): return lax.all_to_all(copies, axis, 0, 0)]
    all_to_all x0 -> x1, waiting for transfers between devices: none -> 8.02 us  [body(): partial = lax.all_to_all(partial, 'row', 0, 0)]
  transfers between devices with their start and end apart: 4 -> 4, of which waited for: 3 -> 2; matrix products, arithmetic and copies ran while one was open for 0% -> 1% of each run, Pallas kernels for 0% -> 0%
where the time goes in v1:
time: 92.8 us; the launch traced here: 92.4 us
  blocking collectives  57.1 us (62%)
  matrix products  12.3 us (13%)
  starting transfers between devices  10.2 us (11%)
  waiting for transfers between devices  9.52 us (10%)
  local copies, waits for them, and re-layouts  1.71 us (2%)
    all_to_all x2, blocking collectives, gather_blocks(): return lax.all_to_all(copies, axis, 0, 0)  38.2 us
    all_to_all x1, blocking collectives, body(): arrived = lax.all_to_all(chunks, 'row', 0, 0)  18.9 us
    all_to_all x1, waiting for transfers between devices, body(): partial = lax.all_to_all(partial, 'row', 0, 0)  8.02 us
    dot_general x1, matrix products, body(): lax.dot_general(vertex_rows, amplitudes, (((0,), (0,)), ((), ())), prefer...  7.63 us
    ppermute x1, starting transfers between devices, body(): rows_other = lax.ppermute(row_block, 'depth', swap)  5.31 us
    dot_general x1, matrix products, body(): lax.dot_general(left, right, (((1,), (1,)), ((), ())), preferred_element_...  4.69 us
    all_to_all x1, starting transfers between devices, body(): partial = lax.all_to_all(partial, 'row', 0, 0)  4.13 us
  transfers between devices with their start and end apart: 4, of which 2 were waited for; matrix products, arithmetic and copies ran while one was open for 1% of the time, Pallas kernels for 0%

profile of v1, /device:TPU:1, one launch (start us, length us, event | category | flops | bytes accessed | tf_op | source)
XLA Modules:
  0.0 92.4 jit_solution(12487365345738070014)
XLA Ops:
  0.6 1.0 %broadcast_in_dim.8 = bf16[8,320,128]{2,1,0:T(8,128)(2,1)S(1)} broadcast(bf16[320,128]{1,0:T(8,128)(2,1)} %bitcast.25), dimensions={1,2} | broadcast | bytes 737280 | tf_op jit(solution)/shard_map/broadcast_in_dim | solution.py:20
  1.6 20.4 %all_to_all.20 = bf16[8,320,128]{2,1,0:T(8,128)(2,1)S(1)} all-to-all(bf16[8,320,128]{2,1,0:T(8,128)(2,1)S(1)} %broadcast_in_dim.8), channel_id=1, replica_groups=mesh['row'=8,'col'=8,'depth'=2] {'col'}, dimensions={0} | all-to-all | bytes 1310720 | tf_op jit(solution)/shard_map/all_to_all | solution.py:21
  22.0 7.6 %convolution_convert_fusion.1 = bf16[2560,128]{1,0:T(8,128)(2,1)} fusion(bf16[2560,2560]{1,0:T(8,128)(2,1)} %param.2, bf16[2560,128]{1,0:T(8,128)(2,1)S(1)} %bitcast.24), kind=kOutput, calls=%fused_computation.1 | convolution fusion | flops 1678049280 | bytes 14417920 | tf_op jit(solution)/shard_map/dot_general | solution.py:34
  29.6 4.1 %all-to-all-start.1 = ((bf16[8,320,128]{2,1,0:T(8,128)(2,1)}), bf16[8,320,128]{2,1,0:T(8,128)(2,1)S(1)}, u32[]{:S(2)}, u32[]{:S(2)}) async-start(bf16[8,320,128]{2,1,0:T(8,128)(2,1)} %bitcast.2), calls=%async_computation.1 | async-start | bytes 1310720 | tf_op jit(solution)/shard_map/all_to_all | solution.py:38
  33.7 0.0 copy-done
  33.8 0.7 collective-permute-start
  34.4 8.0 %all-to-all-done.1 = bf16[8,320,128]{2,1,0:T(8,128)(2,1)S(1)} async-done(((bf16[8,320,128]{2,1,0:T(8,128)(2,1)}), bf16[8,320,128]{2,1,0:T(8,128)(2,1)S(1)}, u32[]{:S(2)}, u32[]{:S(2)}) %all-to-all-start.1) | async-done | bytes 655392 | tf_op jit(solution)/shard_map/all_to_all | solution.py:38
  42.4 0.1 convert_reduce_fusion
  42.5 0.0 collective-permute-done
  42.5 0.1 fusion.7
  42.6 0.2 concatenate.15
  42.8 0.1 broadcast_in_dim.10
  42.9 17.9 %all_to_all.21 = bf16[8,336,128]{2,1,0:T(8,128)(2,1)S(1)} all-to-all(bf16[8,336,128]{2,1,0:T(8,128)(2,1)S(1)} %broadcast_in_dim.10), channel_id=1, replica_groups=mesh['row'=8,'col'=8,'depth'=2] {'col'}, dimensions={0} | all-to-all | bytes 1376256 | tf_op jit(solution)/shard_map/all_to_all | solution.py:21
  60.8 0.2 concatenate.16
  61.0 0.1 broadcast_in_dim.11
  61.1 0.1 pad_maximum_fusion
  61.2 18.9 %all_to_all.22 = bf16[8,656,128]{2,1,0:T(8,128)(2,1)S(1)} all-to-all(bf16[8,656,128]{2,1,0:T(8,128)(2,1)S(1)} %pad_maximum_fusion), channel_id=1, replica_groups=mesh['row'=8,'col'=8,'depth'=2] {'row'}, dimensions={0} | all-to-all | bytes 2686976 | tf_op jit(solution)/shard_map/all_to_all | solution.py:52
  80.1 0.1 fusion.13
  80.2 5.3 %collective-permute-start.1 = (bf16[2560,128]{1,0:T(8,128)(2,1)S(1)}, bf16[2560,128]{1,0:T(8,128)(2,1)S(1)}, u32[]{:S(2)}, u32[]{:S(2)}) collective-permute-start(bf16[2560,128]{1,0:T(8,128)(2,1)S(1)} %bitcast.21), channel_id=1, source_target_pairs={{0,1},{1,0},{2,3},{3,2},{4,5},{5,4},{6,7},{7,6},{8,9},{9,8},{10,11... | collective-permute-start | bytes 1966088 | tf_op jit(solution)/shard_map/ppermute | solution.py:62
  85.6 0.1 collective-permute-start.2
  85.7 0.5 convert_reduce_fusion.1
  86.2 1.5 %collective-permute-done.2 = bf16[1280,128]{1,0:T(8,128)(2,1)S(1)} collective-permute-done((bf16[1280,128]{1,0:T(8,128)(2,1)S(1)}, bf16[1280,128]{1,0:T(8,128)(2,1)S(1)}, u32[]{:S(2)}, u32[]{:S(2)}) %collective-permute-start.2) | collective-permute-done | bytes 327712 | tf_op jit(solution)/shard_map/ppermute | solution.py:61
  87.7 0.0 collective-permute-done.1
  87.8 4.7 %convolution_convert_fusion = bf16[2560,1280]{1,0:T(8,128)(2,1)} fusion(bf16[2560,128]{1,0:T(8,128)(2,1)S(1)} %collective-permute-done.1, bf16[2560,128]{1,0:T(8,128)(2,1)S(1)} %bitcast.22, bf16[1280,128]{1,0:T(8,128)(2,1)S(1)} %collective-permute-done.2, bf16[1280,128]{1,0:T(8,128)(2,1)S(1)} %get-tuple-element.4), kind=kOutput, calls=%fused_computation | convolution fusion | flops 1684930560 | bytes 8519680 | tf_op jit(solution)/shard_map/dot_general | solution.py:65
  (9 shorter events, 0.1 us)
Async XLA Ops:
  22.0 11.8 %copy-start = (bf16[128,320]{0,1:T(8,128)(2,1)S(1)}, bf16[128,320]{0,1:T(8,128)(2,1)}, u32[]{:S(2)}) copy-start(bf16[128,320]{0,1:T(8,128)(2,1)} %param.3) | copy-start | bytes 245764
  29.6 12.8 %all-to-all-start.1 = ((bf16[8,320,128]{2,1,0:T(8,128)(2,1)}), bf16[8,320,128]{2,1,0:T(8,128)(2,1)S(1)}, u32[]{:S(2)}, u32[]{:S(2)}) async-start(bf16[8,320,128]{2,1,0:T(8,128)(2,1)} %bitcast.2), calls=%async_computation.1 | async-start | bytes 1310720 | tf_op jit(solution)/shard_map/all_to_all | solution.py:38
  33.8 8.8 %collective-permute-start = (bf16[320,128]{1,0:T(8,128)(2,1)S(1)}, bf16[320,128]{1,0:T(8,128)(2,1)S(1)}, u32[]{:S(2)}, u32[]{:S(2)}) collective-permute-start(bf16[320,128]{1,0:T(8,128)(2,1)S(1)} %bitcast.26), channel_id=1, source_target_pairs={{0,0},{2,16},{4,32},{6,48},{8,64},{10,80},{12,96},{14,112},{16,2},... | collective-permute-start | bytes 245768 | tf_op jit(solution)/shard_map/ppermute | solution.py:32
  80.2 7.5 %collective-permute-start.1 = (bf16[2560,128]{1,0:T(8,128)(2,1)S(1)}, bf16[2560,128]{1,0:T(8,128)(2,1)S(1)}, u32[]{:S(2)}, u32[]{:S(2)}) collective-permute-start(bf16[2560,128]{1,0:T(8,128)(2,1)S(1)} %bitcast.21), channel_id=1, source_target_pairs={{0,1},{1,0},{2,3},{3,2},{4,5},{5,4},{6,7},{7,6},{8,9},{9,8},{10,11... | collective-permute-start | bytes 1966088 | tf_op jit(solution)/shard_map/ppermute | solution.py:62
  85.6 2.1 %collective-permute-start.2 = (bf16[1280,128]{1,0:T(8,128)(2,1)S(1)}, bf16[1280,128]{1,0:T(8,128)(2,1)S(1)}, u32[]{:S(2)}, u32[]{:S(2)}) collective-permute-start(bf16[1280,128]{1,0:T(8,128)(2,1)S(1)} %get-tuple-element.5), channel_id=1, source_target_pairs={{0,1},{1,0},{2,3},{3,2},{4,5},{5,4},{6,7},{7,6},{8,9},{9,8},{10,11... | collective-permute-start | bytes 983048 | tf_op jit(solution)/shard_map/ppermute | solution.py:61

commit v2 on v1

--- a/solution.py
+++ b/solution.py
@@ -1,10 +1,16 @@
+import functools
+
 import jax
 import jax.numpy as jnp
 from jax import lax
+from jax.experimental import pallas as pl
+from jax.experimental.pallas import tpu as pltpu
 from jax.sharding import PartitionSpec as P
 
 F32 = jnp.float32
 BF16 = jnp.bfloat16
+VMEM = pl.BlockSpec(memory_space=pltpu.VMEM)
+HBM = pl.BlockSpec(memory_space=pltpu.HBM)
 
 
 def split_three(x):
@@ -21,25 +27,98 @@
     return lax.all_to_all(copies, axis, 0, 0)
 
 
+def dressing_kernel(bounds, vertex_ref, amplitudes_ref, out_ref, held_ref, sems):
+    copies = []
+    for at, (low, high) in enumerate(bounds):
+        span = pl.ds(low, high - low)
+        copy = pltpu.make_async_copy(amplitudes_ref.at[:, span], held_ref.at[:, span], sems.at[at])
+        copy.start()
+        copies.append(copy)
+    vertex = vertex_ref[...].T
+    for copy, (low, high) in zip(copies, bounds):
+        copy.wait()
+        part = jnp.dot(vertex, held_ref[:, low:high], preferred_element_type=F32)
+        out_ref[low:high, :] = part.T.astype(BF16)
+
+
+def dressing_part(vertex, amplitudes):
+    pairs, fields = vertex.shape
+    width = amplitudes.shape[1]
+    edges = [0, 256, 512, 1024, 1536, 2048, width]
+    bounds = list(zip(edges[:-1], edges[1:]))
+    return pl.pallas_call(
+        functools.partial(dressing_kernel, bounds),
+        in_specs=[VMEM, HBM],
+        out_specs=VMEM,
+        out_shape=jax.ShapeDtypeStruct((width, fields), BF16),
+        scratch_shapes=[
+            pltpu.VMEM((pairs, width), BF16),
+            pltpu.SemaphoreType.DMA((len(bounds),)),
+        ],
+        cost_estimate=pl.CostEstimate(
+            flops=2 * pairs * fields * width, transcendentals=0, bytes_accessed=2 * pairs * width
+        ),
+        compiler_params=pltpu.CompilerParams(vmem_limit_bytes=52 << 20),
+    )(vertex, amplitudes)
+
+
+def residual_kernel(row_mine, row_other, col_mine, col_other, out_ref, turned):
+    @pl.when(pl.program_id(0) == 0)
+    def _():
+        turned[:128, :] = col_mine[...].T
+        turned[128:, :] = col_other[...].T
+
+    left = jnp.concatenate([row_mine[...], row_other[...]], axis=1)
+    out_ref[...] = jnp.dot(left, turned[...], preferred_element_type=F32).astype(BF16)
+
+
+def residual(row_mine, row_other, col_mine, col_other):
+    pairs, fields = row_mine.shape
+    width = col_mine.shape[0]
+    tile = 640
+    tall = pl.BlockSpec((tile, fields), lambda i: (i, 0))
+    whole = pl.BlockSpec((width, fields), lambda i: (0, 0))
+    return pl.pallas_call(
+        residual_kernel,
+        grid=(pairs // tile,),
+        in_specs=[tall, tall, whole, whole],
+        out_specs=pl.BlockSpec((tile, width), lambda i: (i, 0)),
+        out_shape=jax.ShapeDtypeStruct((pairs, width), BF16),
+        scratch_shapes=[pltpu.VMEM((2 * fields, width), BF16)],
+        cost_estimate=pl.CostEstimate(
+            flops=4 * pairs * fields * width, transcendentals=0, bytes_accessed=2 * pairs * width
+        ),
+        compiler_params=pltpu.CompilerParams(vmem_limit_bytes=40 << 20),
+    )(row_mine, row_other, col_mine, col_other)
+
+
 def body(amplitudes, coulomb_vertex):
     rows = lax.axis_size("row")
     cols = lax.axis_size("col")
     fields, width = coulomb_vertex.shape
+    row_index = lax.axis_index("row")
+    col_index = lax.axis_index("col")
     depth_index = lax.axis_index("depth")
-    across = [(r * cols + c, c * rows + r) for r in range(rows) for c in range(cols)]
 
-    shard = coulomb_vertex.T
-    shard_across = lax.ppermute(shard, ("row", "col"), across)
+    shard, row_index, col_index = lax.optimization_barrier((coulomb_vertex.T, row_index, col_index))
     vertex_rows = gather_blocks(shard, "col").reshape(-1, fields)
-    partial = lax.dot_general(
-        vertex_rows, amplitudes, (((0,), (0,)), ((), ())), preferred_element_type=F32
-    )
-    partial = partial.T.astype(BF16).reshape(rows, width, fields)
+    vertex_rows, row_index, col_index = lax.optimization_barrier((vertex_rows, row_index, col_index))
+
+    def served(c, j):
+        return 2 * (((c & ~1) + 2 - (j >> 1)) & 3) + (j & 1)
+
+    pairs = [
+        (c * cols + j, served(c, j) * cols + c) for c in range(rows) for j in range(cols)
+    ]
+    piece = lax.dynamic_slice_in_dim(vertex_rows, served(row_index, col_index) * width, width, 0)
+    vertex_here = lax.ppermute(piece, ("row", "col"), pairs)
+    partial = dressing_part(vertex_rows, amplitudes).reshape(rows, width, fields)
+    partial, vertex_here = lax.optimization_barrier((partial, vertex_here))
     partial = lax.all_to_all(partial, "row", 0, 0)
     dressing = jnp.sum(partial.astype(F32), axis=0)
-    shard_across = shard_across.astype(F32)
-    factor = jnp.sum(shard_across * dressing, axis=0)
-    dressed = (shard_across + dressing).astype(BF16)
+    vertex_here = vertex_here.astype(F32)
+    factor = jnp.sum(vertex_here * dressing, axis=0)
+    dressed = (vertex_here + dressing).astype(BF16)
 
     pad = jnp.zeros((13, fields), BF16)
     block = jnp.concatenate([dressed, split_three(factor), pad])
@@ -60,12 +139,8 @@
     cols_send = lax.dynamic_slice_in_dim(col_block, (1 - depth_index) * half, half, 0)
     cols_other = lax.ppermute(cols_send, "depth", swap)
     rows_other = lax.ppermute(row_block, "depth", swap)
-    left = jnp.concatenate([row_block, rows_other], axis=1)
-    right = jnp.concatenate([cols_mine, cols_other], axis=1)
-    product = lax.dot_general(
-        left, right, (((1,), (1,)), ((), ())), preferred_element_type=F32
-    )
-    return (product.astype(BF16), structure_factor)
+    cycle_residual = residual(row_block, rows_other, cols_mine, cols_other)
+    return (cycle_residual, structure_factor)
 
 
 def solution(mesh):

time: 92.8 us -> 86.7 us (0.934)
  matrix products: 12.3 us -> 0 us
  Pallas kernels: 0 us -> 9.89 us
  waiting for transfers between devices: 9.52 us -> 1.51 us
  blocking collectives: 57.1 us -> 62.8 us
  starting transfers between devices: 10.2 us -> 8.94 us
    dot_general x2 -> x0, matrix products: 12.3 us -> none  [the longest x1 7.63 us: body(): lax.dot_general(vertex_rows, amplitudes, (((0,), (0,)), ((), ())), prefer...]
    all_to_all x0 -> x1, blocking collectives: none -> 11.8 us  [body(): partial = lax.all_to_all(partial, 'row', 0, 0)]
    pallas_call x0 -> x2, Pallas kernels: none -> 9.89 us  [the longest x1 5.54 us: dressing_part(): pl.pallas_call(functools.partial(dressing_kernel, bounds), in_specs=[VMEM...]
    all_to_all x1 -> x0, waiting for transfers between devices: 8.02 us -> none  [body(): partial = lax.all_to_all(partial, 'row', 0, 0)]
    all_to_all x1 -> x0, starting transfers between devices: 4.13 us -> none  [body(): partial = lax.all_to_all(partial, 'row', 0, 0)]
    all_to_all x2, blocking collectives: 38.2 us -> 34.7 us  [gather_blocks(): return lax.all_to_all(copies, axis, 0, 0)]
    all_to_all x1, blocking collectives: 18.9 us -> 16.4 us  [body(): arrived = lax.all_to_all(chunks, 'row', 0, 0)]
    ppermute x1, starting transfers between devices: 0.67 us -> 2.74 us  [body(): vertex_here = lax.ppermute(piece, ('row', 'col'), pairs)]
  transfers between devices with their start and end apart: 4 -> 3, of which waited for: 2 -> 1; matrix products, arithmetic and copies ran while one was open for 1% -> 1% of each run, Pallas kernels for 0% -> 6%
where the time goes in v2:
time: 86.7 us; the launch traced here: 86.4 us
  blocking collectives  62.8 us (72%)
  Pallas kernels  9.89 us (11%)
  starting transfers between devices  8.94 us (10%)
  local copies, waits for them, and re-layouts  1.7 us (2%)
  waiting for transfers between devices  1.51 us (2%)
    all_to_all x2, blocking collectives, gather_blocks(): return lax.all_to_all(copies, axis, 0, 0)  34.7 us
    all_to_all x1, blocking collectives, body(): arrived = lax.all_to_all(chunks, 'row', 0, 0)  16.4 us
    all_to_all x1, blocking collectives, body(): partial = lax.all_to_all(partial, 'row', 0, 0)  11.8 us
    ppermute x1, starting transfers between devices, body(): rows_other = lax.ppermute(row_block, 'depth', swap)  6.09 us
    pallas_call x1, Pallas kernels, dressing_part(): pl.pallas_call(functools.partial(dressing_kernel, bounds), in_specs=[VMEM...  5.54 us
    pallas_call x1, Pallas kernels, residual(): pl.pallas_call(residual_kernel, grid=(pairs // tile,), in_specs=[tall, ta...  4.34 us
    ppermute x1, starting transfers between devices, body(): vertex_here = lax.ppermute(piece, ('row', 'col'), pairs)  2.74 us
  transfers between devices with their start and end apart: 3, of which 1 were waited for; matrix products, arithmetic and copies ran while one was open for 1% of the time, Pallas kernels for 6%

profile of v2, /device:TPU:1, one launch (start us, length us, event | category | flops | bytes accessed | tf_op | source)
XLA Modules:
  0.0 86.4 jit_solution(4364844994734657581)
XLA Ops:
  0.6 1.0 %broadcast_in_dim.8 = bf16[8,320,128]{2,1,0:T(8,128)(2,1)S(1)} broadcast(bf16[320,128]{1,0:T(8,128)(2,1)} %bitcast.25), dimensions={1,2} | broadcast | bytes 737280 | tf_op jit(solution)/shard_map/broadcast_in_dim | solution.py:26
  1.6 20.4 %all_to_all.20 = bf16[8,320,128]{2,1,0:T(8,128)(2,1)S(1)} all-to-all(bf16[8,320,128]{2,1,0:T(8,128)(2,1)S(1)} %broadcast_in_dim.8), channel_id=1, replica_groups=mesh['row'=8,'col'=8,'depth'=2] {'col'}, dimensions={0} | all-to-all | bytes 1310720 | tf_op jit(solution)/shard_map/all_to_all | solution.py:27
  22.0 2.7 %collective-permute-start = (bf16[320,128]{1,0:T(8,128)(2,1)S(1)}, bf16[320,128]{1,0:T(8,128)(2,1)S(1)}, u32[]{:S(2)}, u32[]{:S(2)}) collective-permute-start(bf16[320,128]{1,0:T(8,128)(2,1)S(1)} %constant_dynamic-slice_fusion.2), channel_id=1, source_target_pairs={{0,64},{2,80},{4,32},{6,48},{8,0},{10,16},{12,96},{14,112},{16,66}... | collective-permute-start | bytes 245768 | tf_op jit(solution)/shard_map/ppermute | solution.py:114
  24.7 5.5 %shard_map.41 = bf16[2560,128]{1,0:T(8,128)(2,1)S(1)} custom-call(bf16[2560,128]{1,0:T(8,128)(2,1)S(1)} %bitcast.20, bf16[2560,2560]{1,0:T(8,128)(2,1)} %amplitudes_ref.1), custom_call_target="tpu_custom_call" | custom-call | flops 1677721600 | bytes 13107200 | tf_op jit(solution)/shard_map/pallas_call | solution.py:49
  30.3 0.0 collective-permute-done
  30.3 11.8 %all_to_all.21 = bf16[8,320,128]{2,1,0:T(8,128)(2,1)S(1)} all-to-all(bf16[8,320,128]{2,1,0:T(8,128)(2,1)S(1)} %bitcast.21), channel_id=1, replica_groups=mesh['row'=8,'col'=8,'depth'=2] {'row'}, dimensions={0} | all-to-all | bytes 1310720 | tf_op jit(solution)/shard_map/all_to_all | solution.py:117
  42.1 0.1 convert_reduce_fusion
  42.2 0.1 fusion.1
  42.2 0.2 concatenate.9
  42.4 0.1 broadcast_in_dim.10
  42.5 14.3 %all_to_all.22 = bf16[8,336,128]{2,1,0:T(8,128)(2,1)S(1)} all-to-all(bf16[8,336,128]{2,1,0:T(8,128)(2,1)S(1)} %broadcast_in_dim.10), channel_id=1, replica_groups=mesh['row'=8,'col'=8,'depth'=2] {'col'}, dimensions={0} | all-to-all | bytes 1376256 | tf_op jit(solution)/shard_map/all_to_all | solution.py:27
  56.8 0.2 concatenate.10
  57.1 0.1 broadcast_in_dim.11
  57.2 0.1 pad_maximum_fusion
  57.3 16.4 %all_to_all.23 = bf16[8,656,128]{2,1,0:T(8,128)(2,1)S(1)} all-to-all(bf16[8,656,128]{2,1,0:T(8,128)(2,1)S(1)} %pad_maximum_fusion), channel_id=1, replica_groups=mesh['row'=8,'col'=8,'depth'=2] {'row'}, dimensions={0} | all-to-all | bytes 2686976 | tf_op jit(solution)/shard_map/all_to_all | solution.py:131
  73.7 0.1 fusion.6
  73.8 6.1 %collective-permute-start.1 = (bf16[2560,128]{1,0:T(8,128)(2,1)S(1)}, bf16[2560,128]{1,0:T(8,128)(2,1)S(1)}, u32[]{:S(2)}, u32[]{:S(2)}) collective-permute-start(bf16[2560,128]{1,0:T(8,128)(2,1)S(1)} %bitcast.22), channel_id=1, source_target_pairs={{0,1},{1,0},{2,3},{3,2},{4,5},{5,4},{6,7},{7,6},{8,9},{9,8},{10,11... | collective-permute-start | bytes 1966088 | tf_op jit(solution)/shard_map/ppermute | solution.py:141
  79.9 0.1 collective-permute-start.2
  80.0 0.5 convert_reduce_fusion.1
  80.6 1.5 %collective-permute-done.2.col_other = bf16[1280,128]{1,0:T(8,128)(2,1)S(1)} collective-permute-done((bf16[1280,128]{1,0:T(8,128)(2,1)S(1)}, bf16[1280,128]{1,0:T(8,128)(2,1)S(1)}, u32[]{:S(2)}, u32[]{:S(2)}) %collective-permute-start.2) | collective-permute-done | bytes 327712 | tf_op jit(solution)/shard_map/ppermute | solution.py:140
  82.1 0.0 collective-permute-done.1.row_other
  82.1 4.3 %shard_map.42 = bf16[2560,1280]{1,0:T(8,128)(2,1)} custom-call(bf16[2560,128]{1,0:T(8,128)(2,1)S(1)} %bitcast.23, bf16[2560,128]{1,0:T(8,128)(2,1)S(1)} %collective-permute-done.1.row_other, bf16[1280,128]{1,0:T(8,128)(2,1)S(1)} %get-tuple-element.21.col_mine, bf16[1280,128]{1,0:T(8,128)(2,1)S(1)} %collective-permute-done.2.col_other), custom_call_target="tpu_custom_call" | custom-call | flops 1677721600 | bytes 6553600 | tf_op jit(solution)/shard_map/pallas_call | solution.py:81
  (7 shorter events, 0.1 us)
Async XLA Ops:
  22.0 8.3 %collective-permute-start = (bf16[320,128]{1,0:T(8,128)(2,1)S(1)}, bf16[320,128]{1,0:T(8,128)(2,1)S(1)}, u32[]{:S(2)}, u32[]{:S(2)}) collective-permute-start(bf16[320,128]{1,0:T(8,128)(2,1)S(1)} %constant_dynamic-slice_fusion.2), channel_id=1, source_target_pairs={{0,64},{2,80},{4,32},{6,48},{8,0},{10,16},{12,96},{14,112},{16,66}... | collective-permute-start | bytes 245768 | tf_op jit(solution)/shard_map/ppermute | solution.py:114
  73.8 8.3 %collective-permute-start.1 = (bf16[2560,128]{1,0:T(8,128)(2,1)S(1)}, bf16[2560,128]{1,0:T(8,128)(2,1)S(1)}, u32[]{:S(2)}, u32[]{:S(2)}) collective-permute-start(bf16[2560,128]{1,0:T(8,128)(2,1)S(1)} %bitcast.22), channel_id=1, source_target_pairs={{0,1},{1,0},{2,3},{3,2},{4,5},{5,4},{6,7},{7,6},{8,9},{9,8},{10,11... | collective-permute-start | bytes 1966088 | tf_op jit(solution)/shard_map/ppermute | solution.py:141
  79.9 2.1 %collective-permute-start.2 = (bf16[1280,128]{1,0:T(8,128)(2,1)S(1)}, bf16[1280,128]{1,0:T(8,128)(2,1)S(1)}, u32[]{:S(2)}, u32[]{:S(2)}) collective-permute-start(bf16[1280,128]{1,0:T(8,128)(2,1)S(1)} %get-tuple-element.20), channel_id=1, source_target_pairs={{0,1},{1,0},{2,3},{3,2},{4,5},{5,4},{6,7},{7,6},{8,9},{9,8},{10,11... | collective-permute-start | bytes 983048 | tf_op jit(solution)/shard_map/ppermute | solution.py:140

commit v3 on v2

--- a/solution.py
+++ b/solution.py
@@ -20,6 +20,10 @@
         parts.append(head.astype(BF16))
         x = x - head
     return jnp.stack(parts)
+
+
+def served_pair(c, pair):
+    return ((c & ~1) + 2 - pair) & 3
 
 
 def gather_blocks(block, axis):
@@ -62,7 +66,7 @@
     )(vertex, amplitudes)
 
 
-def residual_kernel(row_mine, row_other, col_mine, col_other, out_ref, turned):
+def residual_kernel(place_ref, row_mine, row_other, col_mine, col_other, out_ref, turned):
     @pl.when(pl.program_id(0) == 0)
     def _():
         turned[:128, :] = col_mine[...].T
@@ -72,24 +76,43 @@
     out_ref[...] = jnp.dot(left, turned[...], preferred_element_type=F32).astype(BF16)
 
 
-def residual(row_mine, row_other, col_mine, col_other):
+def residual(place, row_mine, row_other, col_mine, col_other):
     pairs, fields = row_mine.shape
     width = col_mine.shape[0]
     tile = 640
-    tall = pl.BlockSpec((tile, fields), lambda i: (i, 0))
-    whole = pl.BlockSpec((width, fields), lambda i: (0, 0))
+    tiles = pairs // tile
+    tall = pl.BlockSpec((tile, fields), lambda i, place: (i, 0))
+    whole = pl.BlockSpec((width, fields), lambda i, place: (0, 0))
     return pl.pallas_call(
         residual_kernel,
-        grid=(pairs // tile,),
-        in_specs=[tall, tall, whole, whole],
-        out_specs=pl.BlockSpec((tile, width), lambda i: (i, 0)),
+        grid_spec=pltpu.PrefetchScalarGridSpec(
+            num_scalar_prefetch=1,
+            grid=(tiles,),
+            in_specs=[tall, tall, whole, whole],
+            out_specs=pl.BlockSpec((tile, width), lambda i, place: (served_pair(place[0], i), 0)),
+            scratch_shapes=[pltpu.VMEM((2 * fields, width), BF16)],
+        ),
         out_shape=jax.ShapeDtypeStruct((pairs, width), BF16),
-        scratch_shapes=[pltpu.VMEM((2 * fields, width), BF16)],
         cost_estimate=pl.CostEstimate(
             flops=4 * pairs * fields * width, transcendentals=0, bytes_accessed=2 * pairs * width
         ),
         compiler_params=pltpu.CompilerParams(vmem_limit_bytes=40 << 20),
-    )(row_mine, row_other, col_mine, col_other)
+    )(place, row_mine, row_other, col_mine, col_other)
+
+
+def settle_kernel(block_ref, out_ref):
+    out_ref[...] = block_ref[...]
+
+
+def settle(block, flops):
+    return pl.pallas_call(
+        settle_kernel,
+        in_specs=[VMEM],
+        out_specs=VMEM,
+        out_shape=jax.ShapeDtypeStruct(block.shape, block.dtype),
+        cost_estimate=pl.CostEstimate(flops=flops, transcendentals=0, bytes_accessed=4 * block.size),
+        compiler_params=pltpu.CompilerParams(vmem_limit_bytes=4 << 20),
+    )(block)
 
 
 def body(amplitudes, coulomb_vertex):
@@ -105,7 +128,7 @@
     vertex_rows, row_index, col_index = lax.optimization_barrier((vertex_rows, row_index, col_index))
 
     def served(c, j):
-        return 2 * (((c & ~1) + 2 - (j >> 1)) & 3) + (j & 1)
+        return 2 * served_pair(c, j >> 1) + (j & 1)
 
     pairs = [
         (c * cols + j, served(c, j) * cols + c) for c in range(rows) for j in range(cols)
@@ -120,26 +143,26 @@
     factor = jnp.sum(vertex_here * dressing, axis=0)
     dressed = (vertex_here + dressing).astype(BF16)
 
+    moved = lax.ppermute(dressed, ("row", "col"), [(there, here) for here, there in pairs])
+    moved = settle(moved, 30_000_000_000)
     pad = jnp.zeros((13, fields), BF16)
     block = jnp.concatenate([dressed, split_three(factor), pad])
-    along = gather_blocks(block, "col")
+    along = gather_blocks(block, "row")
     factor = jnp.sum(along[:, width : width + 3].astype(F32), axis=(0, 1))
-    tail = jnp.concatenate([dressed, split_three(factor), pad])
-    chunks = jnp.concatenate(
-        [along[:, :width], jnp.broadcast_to(tail[None], (rows,) + tail.shape)], axis=1
-    )
-    arrived = lax.all_to_all(chunks, "row", 0, 0)
-    structure_factor = jnp.sum(arrived[:, 2 * width : 2 * width + 3].astype(F32), axis=(0, 1))
-    row_block = arrived[:, :width].reshape(-1, fields)
-    col_block = arrived[:, width : 2 * width].reshape(-1, fields)
-
+    col_block = along[:, :width].reshape(-1, fields)
     half = col_block.shape[0] // 2
     swap = [(0, 1), (1, 0)]
     cols_mine = lax.dynamic_slice_in_dim(col_block, depth_index * half, half, 0)
     cols_send = lax.dynamic_slice_in_dim(col_block, (1 - depth_index) * half, half, 0)
     cols_other = lax.ppermute(cols_send, "depth", swap)
+
+    block = jnp.concatenate([moved, split_three(factor), pad])
+    along = gather_blocks(block, "col")
+    structure_factor = jnp.sum(along[:, width : width + 3].astype(F32), axis=(0, 1))
+    row_block = along[:, :width].reshape(-1, fields)
     rows_other = lax.ppermute(row_block, "depth", swap)
-    cycle_residual = residual(row_block, rows_other, cols_mine, cols_other)
+    place = row_index.reshape(1)
+    cycle_residual = residual(place, row_block, rows_other, cols_mine, cols_other)
     return (cycle_residual, structure_factor)
 
 

time: 86.7 us -> 85.4 us (0.985)
  blocking collectives: 62.8 us -> 46 us
  waiting for transfers between devices: 1.51 us -> 9.39 us
  starting transfers between devices: 8.94 us -> 15.8 us
    all_to_all x1 -> x0, blocking collectives: 16.4 us -> none  [body(): arrived = lax.all_to_all(chunks, 'row', 0, 0)]
    all_to_all x0 -> x1, waiting for transfers between devices: none -> 7.94 us  [gather_blocks(): return lax.all_to_all(copies, axis, 0, 0)]
    all_to_all x0 -> x1, starting transfers between devices: none -> 6.09 us  [gather_blocks(): return lax.all_to_all(copies, axis, 0, 0)]
    broadcast_in_dim x2 -> x3, local copies, waits for them, and re-layouts: 1.06 us -> 2 us  [gather_blocks(): copies = jnp.broadcast_to(block[None], (lax.axis_size(axis),) + block.shape)]
    pallas_call x1 -> x2, Pallas kernels: 4.34 us -> 4.35 us  [the longest x1 4.34 us: residual(): pl.pallas_call(residual_kernel, grid_spec=pltpu.PrefetchScalarGridSpec(nu...]
  transfers between devices with their start and end apart: 3 -> 5, of which waited for: 1 -> 2; matrix products, arithmetic and copies ran while one was open for 1% -> 2% of each run, Pallas kernels for 6% -> 7%
where the time goes in v3:
time: 85.4 us; the launch traced here: 85.1 us
  blocking collectives  46 us (54%)
  starting transfers between devices  15.8 us (19%)
  Pallas kernels  9.89 us (12%)
  waiting for transfers between devices  9.39 us (11%)
  local copies, waits for them, and re-layouts  2.48 us (3%)
    all_to_all x2, blocking collectives, gather_blocks(): return lax.all_to_all(copies, axis, 0, 0)  34.3 us
    all_to_all x1, blocking collectives, body(): partial = lax.all_to_all(partial, 'row', 0, 0)  11.8 us
    all_to_all x1, waiting for transfers between devices, gather_blocks(): return lax.all_to_all(copies, axis, 0, 0)  7.94 us
    ppermute x1, starting transfers between devices, body(): rows_other = lax.ppermute(row_block, 'depth', swap)  6.83 us
    all_to_all x1, starting transfers between devices, gather_blocks(): return lax.all_to_all(copies, axis, 0, 0)  6.09 us
    pallas_call x1, Pallas kernels, dressing_part(): pl.pallas_call(functools.partial(dressing_kernel, bounds), in_specs=[VMEM...  5.54 us
    pallas_call x1, Pallas kernels, residual(): pl.pallas_call(residual_kernel, grid_spec=pltpu.PrefetchScalarGridSpec(nu...  4.34 us
    ppermute x1, starting transfers between devices, body(): vertex_here = lax.ppermute(piece, ('row', 'col'), pairs)  2.74 us
  transfers between devices with their start and end apart: 5, of which 2 were waited for; matrix products, arithmetic and copies ran while one was open for 2% of the time, Pallas kernels for 7%

profile of v3, /device:TPU:1, one launch (start us, length us, event | category | flops | bytes accessed | tf_op | source)
XLA Modules:
  0.0 85.1 jit_solution(8183662806398730615)
XLA Ops:
  0.6 1.0 %broadcast_in_dim.8 = bf16[8,320,128]{2,1,0:T(8,128)(2,1)S(1)} broadcast(bf16[320,128]{1,0:T(8,128)(2,1)} %bitcast.26), dimensions={1,2} | broadcast | bytes 737280 | tf_op jit(solution)/shard_map/broadcast_in_dim | solution.py:30
  1.6 20.4 %all_to_all.20 = bf16[8,320,128]{2,1,0:T(8,128)(2,1)S(1)} all-to-all(bf16[8,320,128]{2,1,0:T(8,128)(2,1)S(1)} %broadcast_in_dim.8), channel_id=1, replica_groups=mesh['row'=8,'col'=8,'depth'=2] {'col'}, dimensions={0} | all-to-all | bytes 1310720 | tf_op jit(solution)/shard_map/all_to_all | solution.py:31
  22.0 2.7 %collective-permute-start = (bf16[320,128]{1,0:T(8,128)(2,1)S(1)}, bf16[320,128]{1,0:T(8,128)(2,1)S(1)}, u32[]{:S(2)}, u32[]{:S(2)}) collective-permute-start(bf16[320,128]{1,0:T(8,128)(2,1)S(1)} %constant_dynamic-slice_fusion.2), channel_id=1, source_target_pairs={{0,64},{2,80},{4,32},{6,48},{8,0},{10,16},{12,96},{14,112},{16,66}... | collective-permute-start | bytes 245768 | tf_op jit(solution)/shard_map/ppermute | solution.py:137
  24.7 5.5 %shard_map.41 = bf16[2560,128]{1,0:T(8,128)(2,1)S(1)} custom-call(bf16[2560,128]{1,0:T(8,128)(2,1)S(1)} %bitcast.21, bf16[2560,2560]{1,0:T(8,128)(2,1)} %amplitudes_ref.1), custom_call_target="tpu_custom_call" | custom-call | flops 1677721600 | bytes 13107200 | tf_op jit(solution)/shard_map/pallas_call | solution.py:53
  30.3 0.0 collective-permute-done
  30.3 11.8 %all_to_all.21 = bf16[8,320,128]{2,1,0:T(8,128)(2,1)S(1)} all-to-all(bf16[8,320,128]{2,1,0:T(8,128)(2,1)S(1)} %bitcast.22), channel_id=1, replica_groups=mesh['row'=8,'col'=8,'depth'=2] {'row'}, dimensions={0} | all-to-all | bytes 1310720 | tf_op jit(solution)/shard_map/all_to_all | solution.py:140
  42.1 0.1 convert_reduce_fusion
  42.2 0.1 fusion.1
  42.2 0.1 collective-permute-start.1
  42.3 0.2 concatenate.6
  42.5 0.9 %broadcast_in_dim.10 = bf16[8,336,128]{2,1,0:T(8,128)(2,1)} broadcast(bf16[336,128]{1,0:T(8,128)(2,1)S(1)} %concatenate.6), dimensions={1,2} | broadcast | bytes 774144 | tf_op jit(solution)/shard_map/broadcast_in_dim | solution.py:30
  43.4 6.1 %all-to-all-start.2 = ((bf16[8,336,128]{2,1,0:T(8,128)(2,1)}), bf16[8,336,128]{2,1,0:T(8,128)(2,1)S(1)}, u32[]{:S(2)}, u32[]{:S(2)}) async-start(bf16[8,336,128]{2,1,0:T(8,128)(2,1)} %broadcast_in_dim.10), calls=%async_computation.2 | async-start | bytes 1376256 | tf_op jit(solution)/shard_map/all_to_all | solution.py:31
  49.5 0.0 collective-permute-done.1.block_ref
  49.5 7.9 %all-to-all-done.2 = bf16[8,336,128]{2,1,0:T(8,128)(2,1)S(1)} async-done(((bf16[8,336,128]{2,1,0:T(8,128)(2,1)}), bf16[8,336,128]{2,1,0:T(8,128)(2,1)S(1)}, u32[]{:S(2)}, u32[]{:S(2)}) %all-to-all-start.2) | async-done | bytes 688160 | tf_op jit(solution)/shard_map/all_to_all | solution.py:31
  57.5 0.2 concatenate.7
  57.7 0.1 broadcast_in_dim.11
  57.8 13.9 %all_to_all.22 = bf16[8,336,128]{2,1,0:T(8,128)(2,1)S(1)} all-to-all(bf16[8,336,128]{2,1,0:T(8,128)(2,1)S(1)} %broadcast_in_dim.11), channel_id=1, replica_groups=mesh['row'=8,'col'=8,'depth'=2] {'col'}, dimensions={0} | all-to-all | bytes 1376256 | tf_op jit(solution)/shard_map/all_to_all | solution.py:31
  71.7 6.8 %collective-permute-start.2 = (bf16[2560,128]{1,0:T(8,128)(2,1)S(1)}, bf16[2560,128]{1,0:T(8,128)(2,1)S(1)}, u32[]{:S(2)}, u32[]{:S(2)}) collective-permute-start(bf16[2560,128]{1,0:T(8,128)(2,1)S(1)} %bitcast.23), channel_id=1, source_target_pairs={{0,1},{1,0},{2,3},{3,2},{4,5},{5,4},{6,7},{7,6},{8,9},{9,8},{10,11... | collective-permute-start | bytes 1966088 | tf_op jit(solution)/shard_map/ppermute | solution.py:163
  78.6 0.1 constant_dynamic-slice_fusion
  78.7 0.1 collective-permute-start.3
  78.8 0.5 convert_reduce_fusion.1
  79.3 1.4 %collective-permute-done.3.col_other = bf16[1280,128]{1,0:T(8,128)(2,1)S(1)} collective-permute-done((bf16[1280,128]{1,0:T(8,128)(2,1)S(1)}, bf16[1280,128]{1,0:T(8,128)(2,1)S(1)}, u32[]{:S(2)}, u32[]{:S(2)}) %collective-permute-start.3) | collective-permute-done | bytes 327712 | tf_op jit(solution)/shard_map/ppermute | solution.py:157
  80.7 0.0 collective-permute-done.2.row_other
  80.7 4.3 %shard_map.43 = bf16[2560,1280]{1,0:T(8,128)(2,1)} custom-call(s32[1]{0:T(128)} %bitcast.2.place_ref, bf16[2560,128]{1,0:T(8,128)(2,1)S(1)} %bitcast.24, bf16[2560,128]{1,0:T(8,128)(2,1)S(1)} %collective-permute-done.2.row_other, bf16[1280,128]{1,0:T(8,128)(2,1)S(1)} %get-tuple-element.19.col_mine, bf16[1280,128]{1,0:T(8,128)(2,1)S(1)} %collective-permute-done.3.col_other), custom_call_target="tpu_custom_call" | custom-call | flops 1677721600 | bytes 6553600 | tf_op jit(solution)/shard_map/pallas_call | solution.py:86
  (8 shorter events, 0.1 us)
Async XLA Ops:
  22.0 8.3 %collective-permute-start = (bf16[320,128]{1,0:T(8,128)(2,1)S(1)}, bf16[320,128]{1,0:T(8,128)(2,1)S(1)}, u32[]{:S(2)}, u32[]{:S(2)}) collective-permute-start(bf16[320,128]{1,0:T(8,128)(2,1)S(1)} %constant_dynamic-slice_fusion.2), channel_id=1, source_target_pairs={{0,64},{2,80},{4,32},{6,48},{8,0},{10,16},{12,96},{14,112},{16,66}... | collective-permute-start | bytes 245768 | tf_op jit(solution)/shard_map/ppermute | solution.py:137
  42.2 7.3 %collective-permute-start.1 = (bf16[320,128]{1,0:T(8,128)(2,1)S(1)}, bf16[320,128]{1,0:T(8,128)(2,1)S(1)}, u32[]{:S(2)}, u32[]{:S(2)}) collective-permute-start(bf16[320,128]{1,0:T(8,128)(2,1)S(1)} %get-tuple-element.21), channel_id=1, source_target_pairs={{64,0},{80,2},{32,4},{48,6},{0,8},{16,10},{96,12},{112,14},{66,16}... | collective-permute-start | bytes 245768 | tf_op jit(solution)/shard_map/ppermute | solution.py:146
  43.4 14.1 %all-to-all-start.2 = ((bf16[8,336,128]{2,1,0:T(8,128)(2,1)}), bf16[8,336,128]{2,1,0:T(8,128)(2,1)S(1)}, u32[]{:S(2)}, u32[]{:S(2)}) async-start(bf16[8,336,128]{2,1,0:T(8,128)(2,1)} %broadcast_in_dim.10), calls=%async_computation.2 | async-start | bytes 1376256 | tf_op jit(solution)/shard_map/all_to_all | solution.py:31
  71.7 9.0 %collective-permute-start.2 = (bf16[2560,128]{1,0:T(8,128)(2,1)S(1)}, bf16[2560,128]{1,0:T(8,128)(2,1)S(1)}, u32[]{:S(2)}, u32[]{:S(2)}) collective-permute-start(bf16[2560,128]{1,0:T(8,128)(2,1)S(1)} %bitcast.23), channel_id=1, source_target_pairs={{0,1},{1,0},{2,3},{3,2},{4,5},{5,4},{6,7},{7,6},{8,9},{9,8},{10,11... | collective-permute-start | bytes 1966088 | tf_op jit(solution)/shard_map/ppermute | solution.py:163
  78.7 2.1 %collective-permute-start.3 = (bf16[1280,128]{1,0:T(8,128)(2,1)S(1)}, bf16[1280,128]{1,0:T(8,128)(2,1)S(1)}, u32[]{:S(2)}, u32[]{:S(2)}) collective-permute-start(bf16[1280,128]{1,0:T(8,128)(2,1)S(1)} %get-tuple-element.18), channel_id=1, source_target_pairs={{0,1},{1,0},{2,3},{3,2},{4,5},{5,4},{6,7},{7,6},{8,9},{9,8},{10,11... | collective-permute-start | bytes 983048 | tf_op jit(solution)/shard_map/ppermute | solution.py:157

commit v4 on v3

--- a/solution.py
+++ b/solution.py
@@ -10,6 +10,7 @@
 F32 = jnp.float32
 BF16 = jnp.bfloat16
 VMEM = pl.BlockSpec(memory_space=pltpu.VMEM)
+SMEM = pl.BlockSpec(memory_space=pltpu.SMEM)
 HBM = pl.BlockSpec(memory_space=pltpu.HBM)
 
 
@@ -66,33 +67,38 @@
     )(vertex, amplitudes)
 
 
-def residual_kernel(place_ref, row_mine, row_other, col_mine, col_other, out_ref, turned):
-    @pl.when(pl.program_id(0) == 0)
-    def _():
-        turned[:128, :] = col_mine[...].T
-        turned[128:, :] = col_other[...].T
-
-    left = jnp.concatenate([row_mine[...], row_other[...]], axis=1)
-    out_ref[...] = jnp.dot(left, turned[...], preferred_element_type=F32).astype(BF16)
+def residual_kernel(place_ref, row_mine, row_other, col_mine, col_other, out_ref, turned, stage, sems):
+    fields = row_mine.shape[1]
+    tiles, tile, _ = stage.shape
+    turned[:fields, :] = col_mine[...].T
+    turned[fields:, :] = col_other[...].T
+    copies = []
+    for at in range(tiles):
+        span = slice(at * tile, (at + 1) * tile)
+        left = jnp.concatenate([row_mine[span, :], row_other[span, :]], axis=1)
+        stage[at] = jnp.dot(left, turned[...], preferred_element_type=F32).astype(BF16)
+        to = pl.multiple_of(served_pair(place_ref[0], at) * tile, 128)
+        copy = pltpu.make_async_copy(stage.at[at], out_ref.at[pl.ds(to, tile), :], sems.at[at])
+        copy.start()
+        copies.append(copy)
+    for copy in copies:
+        copy.wait()
 
 
 def residual(place, row_mine, row_other, col_mine, col_other):
     pairs, fields = row_mine.shape
     width = col_mine.shape[0]
-    tile = 640
-    tiles = pairs // tile
-    tall = pl.BlockSpec((tile, fields), lambda i, place: (i, 0))
-    whole = pl.BlockSpec((width, fields), lambda i, place: (0, 0))
+    tiles = 4
     return pl.pallas_call(
         residual_kernel,
-        grid_spec=pltpu.PrefetchScalarGridSpec(
-            num_scalar_prefetch=1,
-            grid=(tiles,),
-            in_specs=[tall, tall, whole, whole],
-            out_specs=pl.BlockSpec((tile, width), lambda i, place: (served_pair(place[0], i), 0)),
-            scratch_shapes=[pltpu.VMEM((2 * fields, width), BF16)],
-        ),
+        in_specs=[SMEM, VMEM, VMEM, VMEM, VMEM],
+        out_specs=HBM,
         out_shape=jax.ShapeDtypeStruct((pairs, width), BF16),
+        scratch_shapes=[
+            pltpu.VMEM((2 * fields, width), BF16),
+            pltpu.VMEM((tiles, pairs // tiles, width), BF16),
+            pltpu.SemaphoreType.DMA((tiles,)),
+        ],
         cost_estimate=pl.CostEstimate(
             flops=4 * pairs * fields * width, transcendentals=0, bytes_accessed=2 * pairs * width
         ),

time: 85.4 us -> 84.7 us (level)
  no operation moved by 1% of the time
where the time goes in v4:
time: 84.7 us; the launch traced here: 84.3 us
  blocking collectives  46 us (54%)
  starting transfers between devices  15.8 us (19%)
  waiting for transfers between devices  9.39 us (11%)
  Pallas kernels  9.14 us (11%)
  local copies, waits for them, and re-layouts  2.48 us (3%)
    all_to_all x2, blocking collectives, gather_blocks(): return lax.all_to_all(copies, axis, 0, 0)  34.3 us
    all_to_all x1, blocking collectives, body(): partial = lax.all_to_all(partial, 'row', 0, 0)  11.8 us
    all_to_all x1, waiting for transfers between devices, gather_blocks(): return lax.all_to_all(copies, axis, 0, 0)  7.94 us
    ppermute x1, starting transfers between devices, body(): rows_other = lax.ppermute(row_block, 'depth', swap)  6.83 us
    all_to_all x1, starting transfers between devices, gather_blocks(): return lax.all_to_all(copies, axis, 0, 0)  6.09 us
    pallas_call x1, Pallas kernels, dressing_part(): pl.pallas_call(functools.partial(dressing_kernel, bounds), in_specs=[VMEM...  5.54 us
    pallas_call x1, Pallas kernels, residual(): pl.pallas_call(residual_kernel, in_specs=[SMEM, VMEM, VMEM, VMEM, VMEM],...  3.59 us
    ppermute x1, starting transfers between devices, body(): vertex_here = lax.ppermute(piece, ('row', 'col'), pairs)  2.74 us
  transfers between devices with their start and end apart: 5, of which 2 were waited for; matrix products, arithmetic and copies ran while one was open for 2% of the time, Pallas kernels for 7%

profile of v4, /device:TPU:1, one launch (start us, length us, event | category | flops | bytes accessed | tf_op | source)
XLA Modules:
  0.0 84.3 jit_solution(1309489602691762491)
XLA Ops:
  0.6 1.0 %broadcast_in_dim.8 = bf16[8,320,128]{2,1,0:T(8,128)(2,1)S(1)} broadcast(bf16[320,128]{1,0:T(8,128)(2,1)} %bitcast.26), dimensions={1,2} | broadcast | bytes 737280 | tf_op jit(solution)/shard_map/broadcast_in_dim | solution.py:31
  1.6 20.4 %all_to_all.20 = bf16[8,320,128]{2,1,0:T(8,128)(2,1)S(1)} all-to-all(bf16[8,320,128]{2,1,0:T(8,128)(2,1)S(1)} %broadcast_in_dim.8), channel_id=1, replica_groups=mesh['row'=8,'col'=8,'depth'=2] {'col'}, dimensions={0} | all-to-all | bytes 1310720 | tf_op jit(solution)/shard_map/all_to_all | solution.py:32
  22.0 2.7 %collective-permute-start = (bf16[320,128]{1,0:T(8,128)(2,1)S(1)}, bf16[320,128]{1,0:T(8,128)(2,1)S(1)}, u32[]{:S(2)}, u32[]{:S(2)}) collective-permute-start(bf16[320,128]{1,0:T(8,128)(2,1)S(1)} %constant_dynamic-slice_fusion.2), channel_id=1, source_target_pairs={{0,64},{2,80},{4,32},{6,48},{8,0},{10,16},{12,96},{14,112},{16,66}... | collective-permute-start | bytes 245768 | tf_op jit(solution)/shard_map/ppermute | solution.py:143
  24.7 5.5 %shard_map.41 = bf16[2560,128]{1,0:T(8,128)(2,1)S(1)} custom-call(bf16[2560,128]{1,0:T(8,128)(2,1)S(1)} %bitcast.21, bf16[2560,2560]{1,0:T(8,128)(2,1)} %amplitudes_ref.1), custom_call_target="tpu_custom_call" | custom-call | flops 1677721600 | bytes 13107200 | tf_op jit(solution)/shard_map/pallas_call | solution.py:54
  30.3 0.0 collective-permute-done
  30.3 11.8 %all_to_all.21 = bf16[8,320,128]{2,1,0:T(8,128)(2,1)S(1)} all-to-all(bf16[8,320,128]{2,1,0:T(8,128)(2,1)S(1)} %bitcast.22), channel_id=1, replica_groups=mesh['row'=8,'col'=8,'depth'=2] {'row'}, dimensions={0} | all-to-all | bytes 1310720 | tf_op jit(solution)/shard_map/all_to_all | solution.py:146
  42.1 0.1 convert_reduce_fusion
  42.2 0.1 fusion.1
  42.2 0.1 collective-permute-start.1
  42.3 0.2 concatenate.6
  42.5 0.9 %broadcast_in_dim.10 = bf16[8,336,128]{2,1,0:T(8,128)(2,1)} broadcast(bf16[336,128]{1,0:T(8,128)(2,1)S(1)} %concatenate.6), dimensions={1,2} | broadcast | bytes 774144 | tf_op jit(solution)/shard_map/broadcast_in_dim | solution.py:31
  43.4 6.1 %all-to-all-start.2 = ((bf16[8,336,128]{2,1,0:T(8,128)(2,1)}), bf16[8,336,128]{2,1,0:T(8,128)(2,1)S(1)}, u32[]{:S(2)}, u32[]{:S(2)}) async-start(bf16[8,336,128]{2,1,0:T(8,128)(2,1)} %broadcast_in_dim.10), calls=%async_computation.2 | async-start | bytes 1376256 | tf_op jit(solution)/shard_map/all_to_all | solution.py:32
  49.5 0.0 collective-permute-done.1.block_ref
  49.5 7.9 %all-to-all-done.2 = bf16[8,336,128]{2,1,0:T(8,128)(2,1)S(1)} async-done(((bf16[8,336,128]{2,1,0:T(8,128)(2,1)}), bf16[8,336,128]{2,1,0:T(8,128)(2,1)S(1)}, u32[]{:S(2)}, u32[]{:S(2)}) %all-to-all-start.2) | async-done | bytes 688160 | tf_op jit(solution)/shard_map/all_to_all | solution.py:32
  57.5 0.2 concatenate.7
  57.7 0.1 broadcast_in_dim.11
  57.8 13.9 %all_to_all.22 = bf16[8,336,128]{2,1,0:T(8,128)(2,1)S(1)} all-to-all(bf16[8,336,128]{2,1,0:T(8,128)(2,1)S(1)} %broadcast_in_dim.11), channel_id=1, replica_groups=mesh['row'=8,'col'=8,'depth'=2] {'col'}, dimensions={0} | all-to-all | bytes 1376256 | tf_op jit(solution)/shard_map/all_to_all | solution.py:32
  71.7 6.8 %collective-permute-start.2 = (bf16[2560,128]{1,0:T(8,128)(2,1)S(1)}, bf16[2560,128]{1,0:T(8,128)(2,1)S(1)}, u32[]{:S(2)}, u32[]{:S(2)}) collective-permute-start(bf16[2560,128]{1,0:T(8,128)(2,1)S(1)} %bitcast.23), channel_id=1, source_target_pairs={{0,1},{1,0},{2,3},{3,2},{4,5},{5,4},{6,7},{7,6},{8,9},{9,8},{10,11... | collective-permute-start | bytes 1966088 | tf_op jit(solution)/shard_map/ppermute | solution.py:169
  78.6 0.1 constant_dynamic-slice_fusion
  78.7 0.1 collective-permute-start.3
  78.8 0.5 convert_reduce_fusion.1
  79.3 1.4 %collective-permute-done.3.col_other = bf16[1280,128]{1,0:T(8,128)(2,1)S(1)} collective-permute-done((bf16[1280,128]{1,0:T(8,128)(2,1)S(1)}, bf16[1280,128]{1,0:T(8,128)(2,1)S(1)}, u32[]{:S(2)}, u32[]{:S(2)}) %collective-permute-start.3) | collective-permute-done | bytes 327712 | tf_op jit(solution)/shard_map/ppermute | solution.py:163
  80.7 0.0 collective-permute-done.2.row_other
  80.7 3.6 %shard_map.43 = bf16[2560,1280]{1,0:T(8,128)(2,1)} custom-call(s32[1]{0:T(128)} %bitcast.2.place_ref, bf16[2560,128]{1,0:T(8,128)(2,1)S(1)} %bitcast.24, bf16[2560,128]{1,0:T(8,128)(2,1)S(1)} %collective-permute-done.2.row_other, bf16[1280,128]{1,0:T(8,128)(2,1)S(1)} %get-tuple-element.19.col_mine, bf16[1280,128]{1,0:T(8,128)(2,1)S(1)} %collective-permute-done.3.col_other), custom_call_target="tpu_custom_call" | custom-call | flops 1677721600 | bytes 6553600 | tf_op jit(solution)/shard_map/pallas_call | solution.py:92
  (8 shorter events, 0.1 us)
Async XLA Ops:
  22.0 8.3 %collective-permute-start = (bf16[320,128]{1,0:T(8,128)(2,1)S(1)}, bf16[320,128]{1,0:T(8,128)(2,1)S(1)}, u32[]{:S(2)}, u32[]{:S(2)}) collective-permute-start(bf16[320,128]{1,0:T(8,128)(2,1)S(1)} %constant_dynamic-slice_fusion.2), channel_id=1, source_target_pairs={{0,64},{2,80},{4,32},{6,48},{8,0},{10,16},{12,96},{14,112},{16,66}... | collective-permute-start | bytes 245768 | tf_op jit(solution)/shard_map/ppermute | solution.py:143
  42.2 7.3 %collective-permute-start.1 = (bf16[320,128]{1,0:T(8,128)(2,1)S(1)}, bf16[320,128]{1,0:T(8,128)(2,1)S(1)}, u32[]{:S(2)}, u32[]{:S(2)}) collective-permute-start(bf16[320,128]{1,0:T(8,128)(2,1)S(1)} %get-tuple-element.21), channel_id=1, source_target_pairs={{64,0},{80,2},{32,4},{48,6},{0,8},{16,10},{96,12},{112,14},{66,16}... | collective-permute-start | bytes 245768 | tf_op jit(solution)/shard_map/ppermute | solution.py:152
  43.4 14.1 %all-to-all-start.2 = ((bf16[8,336,128]{2,1,0:T(8,128)(2,1)}), bf16[8,336,128]{2,1,0:T(8,128)(2,1)S(1)}, u32[]{:S(2)}, u32[]{:S(2)}) async-start(bf16[8,336,128]{2,1,0:T(8,128)(2,1)} %broadcast_in_dim.10), calls=%async_computation.2 | async-start | bytes 1376256 | tf_op jit(solution)/shard_map/all_to_all | solution.py:32
  71.7 9.0 %collective-permute-start.2 = (bf16[2560,128]{1,0:T(8,128)(2,1)S(1)}, bf16[2560,128]{1,0:T(8,128)(2,1)S(1)}, u32[]{:S(2)}, u32[]{:S(2)}) collective-permute-start(bf16[2560,128]{1,0:T(8,128)(2,1)S(1)} %bitcast.23), channel_id=1, source_target_pairs={{0,1},{1,0},{2,3},{3,2},{4,5},{5,4},{6,7},{7,6},{8,9},{9,8},{10,11... | collective-permute-start | bytes 1966088 | tf_op jit(solution)/shard_map/ppermute | solution.py:169
  78.7 2.1 %collective-permute-start.3 = (bf16[1280,128]{1,0:T(8,128)(2,1)S(1)}, bf16[1280,128]{1,0:T(8,128)(2,1)S(1)}, u32[]{:S(2)}, u32[]{:S(2)}) collective-permute-start(bf16[1280,128]{1,0:T(8,128)(2,1)S(1)} %get-tuple-element.18), channel_id=1, source_target_pairs={{0,1},{1,0},{2,3},{3,2},{4,5},{5,4},{6,7},{7,6},{8,9},{9,8},{10,11... | collective-permute-start | bytes 983048 | tf_op jit(solution)/shard_map/ppermute | solution.py:163

commit v5 on v4

--- a/solution.py
+++ b/solution.py
@@ -151,7 +151,7 @@
 
     moved = lax.ppermute(dressed, ("row", "col"), [(there, here) for here, there in pairs])
     moved = settle(moved, 30_000_000_000)
-    pad = jnp.zeros((13, fields), BF16)
+    pad = jnp.zeros((5, fields), BF16)
     block = jnp.concatenate([dressed, split_three(factor), pad])
     along = gather_blocks(block, "row")
     factor = jnp.sum(along[:, width : width + 3].astype(F32), axis=(0, 1))

time: 84.7 us -> 84.3 us (level)
  no operation moved by 1% of the time
where the time goes in v5:
time: 84.3 us; the launch traced here: 84 us
  blocking collectives  46 us (55%)
  starting transfers between devices  15.8 us (19%)
  waiting for transfers between devices  9.32 us (11%)
  Pallas kernels  9.14 us (11%)
  local copies, waits for them, and re-layouts  2.24 us (3%)
    all_to_all x2, blocking collectives, gather_blocks(): return lax.all_to_all(copies, axis, 0, 0)  34.2 us
    all_to_all x1, blocking collectives, body(): partial = lax.all_to_all(partial, 'row', 0, 0)  11.8 us
    all_to_all x1, waiting for transfers between devices, gather_blocks(): return lax.all_to_all(copies, axis, 0, 0)  7.86 us
    ppermute x1, starting transfers between devices, body(): rows_other = lax.ppermute(row_block, 'depth', swap)  6.84 us
    all_to_all x1, starting transfers between devices, gather_blocks(): return lax.all_to_all(copies, axis, 0, 0)  6.09 us
    pallas_call x1, Pallas kernels, dressing_part(): pl.pallas_call(functools.partial(dressing_kernel, bounds), in_specs=[VMEM...  5.54 us
    pallas_call x1, Pallas kernels, residual(): pl.pallas_call(residual_kernel, in_specs=[SMEM, VMEM, VMEM, VMEM, VMEM],...  3.59 us
    ppermute x1, starting transfers between devices, body(): vertex_here = lax.ppermute(piece, ('row', 'col'), pairs)  2.74 us
  transfers between devices with their start and end apart: 5, of which 2 were waited for; matrix products, arithmetic and copies ran while one was open for 2% of the time, Pallas kernels for 7%

profile of v5, /device:TPU:1, one launch (start us, length us, event | category | flops | bytes accessed | tf_op | source)
XLA Modules:
  0.0 84.0 jit_solution(16547770555978278880)
XLA Ops:
  0.6 1.0 %broadcast_in_dim.8 = bf16[8,320,128]{2,1,0:T(8,128)(2,1)S(1)} broadcast(bf16[320,128]{1,0:T(8,128)(2,1)} %bitcast.26), dimensions={1,2} | broadcast | bytes 737280 | tf_op jit(solution)/shard_map/broadcast_in_dim | solution.py:31
  1.6 20.4 %all_to_all.20 = bf16[8,320,128]{2,1,0:T(8,128)(2,1)S(1)} all-to-all(bf16[8,320,128]{2,1,0:T(8,128)(2,1)S(1)} %broadcast_in_dim.8), channel_id=1, replica_groups=mesh['row'=8,'col'=8,'depth'=2] {'col'}, dimensions={0} | all-to-all | bytes 1310720 | tf_op jit(solution)/shard_map/all_to_all | solution.py:32
  22.0 2.7 %collective-permute-start = (bf16[320,128]{1,0:T(8,128)(2,1)S(1)}, bf16[320,128]{1,0:T(8,128)(2,1)S(1)}, u32[]{:S(2)}, u32[]{:S(2)}) collective-permute-start(bf16[320,128]{1,0:T(8,128)(2,1)S(1)} %constant_dynamic-slice_fusion.2), channel_id=1, source_target_pairs={{0,64},{2,80},{4,32},{6,48},{8,0},{10,16},{12,96},{14,112},{16,66}... | collective-permute-start | bytes 245768 | tf_op jit(solution)/shard_map/ppermute | solution.py:143
  24.7 5.5 %shard_map.41 = bf16[2560,128]{1,0:T(8,128)(2,1)S(1)} custom-call(bf16[2560,128]{1,0:T(8,128)(2,1)S(1)} %bitcast.21, bf16[2560,2560]{1,0:T(8,128)(2,1)} %amplitudes_ref.1), custom_call_target="tpu_custom_call" | custom-call | flops 1677721600 | bytes 13107200 | tf_op jit(solution)/shard_map/pallas_call | solution.py:54
  30.3 0.0 collective-permute-done
  30.3 11.8 %all_to_all.21 = bf16[8,320,128]{2,1,0:T(8,128)(2,1)S(1)} all-to-all(bf16[8,320,128]{2,1,0:T(8,128)(2,1)S(1)} %bitcast.22), channel_id=1, replica_groups=mesh['row'=8,'col'=8,'depth'=2] {'row'}, dimensions={0} | all-to-all | bytes 1310720 | tf_op jit(solution)/shard_map/all_to_all | solution.py:146
  42.1 0.1 convert_reduce_fusion
  42.2 0.1 fusion.1
  42.2 0.1 collective-permute-start.1
  42.3 0.1 concatenate.6
  42.4 0.9 %broadcast_in_dim.10 = bf16[8,328,128]{2,1,0:T(8,128)(2,1)} broadcast(bf16[328,128]{1,0:T(8,128)(2,1)S(1)} %concatenate.6), dimensions={1,2} | broadcast | bytes 755712 | tf_op jit(solution)/shard_map/broadcast_in_dim | solution.py:31
  43.3 6.1 %all-to-all-start.2 = ((bf16[8,328,128]{2,1,0:T(8,128)(2,1)}), bf16[8,328,128]{2,1,0:T(8,128)(2,1)S(1)}, u32[]{:S(2)}, u32[]{:S(2)}) async-start(bf16[8,328,128]{2,1,0:T(8,128)(2,1)} %broadcast_in_dim.10), calls=%async_computation.2 | async-start | bytes 1343488 | tf_op jit(solution)/shard_map/all_to_all | solution.py:32
  49.4 0.0 collective-permute-done.1.block_ref
  49.4 7.9 %all-to-all-done.2 = bf16[8,328,128]{2,1,0:T(8,128)(2,1)S(1)} async-done(((bf16[8,328,128]{2,1,0:T(8,128)(2,1)}), bf16[8,328,128]{2,1,0:T(8,128)(2,1)S(1)}, u32[]{:S(2)}, u32[]{:S(2)}) %all-to-all-start.2) | async-done | bytes 671776 | tf_op jit(solution)/shard_map/all_to_all | solution.py:32
  57.3 0.1 concatenate.7
  57.4 0.1 broadcast_in_dim.11
  57.5 13.8 %all_to_all.22 = bf16[8,328,128]{2,1,0:T(8,128)(2,1)S(1)} all-to-all(bf16[8,328,128]{2,1,0:T(8,128)(2,1)S(1)} %broadcast_in_dim.11), channel_id=1, replica_groups=mesh['row'=8,'col'=8,'depth'=2] {'col'}, dimensions={0} | all-to-all | bytes 1343488 | tf_op jit(solution)/shard_map/all_to_all | solution.py:32
  71.3 6.8 %collective-permute-start.2 = (bf16[2560,128]{1,0:T(8,128)(2,1)S(1)}, bf16[2560,128]{1,0:T(8,128)(2,1)S(1)}, u32[]{:S(2)}, u32[]{:S(2)}) collective-permute-start(bf16[2560,128]{1,0:T(8,128)(2,1)S(1)} %bitcast.23), channel_id=1, source_target_pairs={{0,1},{1,0},{2,3},{3,2},{4,5},{5,4},{6,7},{7,6},{8,9},{9,8},{10,11... | collective-permute-start | bytes 1966088 | tf_op jit(solution)/shard_map/ppermute | solution.py:169
  78.2 0.1 constant_dynamic-slice_fusion
  78.3 0.1 collective-permute-start.3
  78.4 0.5 convert_reduce_fusion.1
  78.9 1.4 %collective-permute-done.3.col_other = bf16[1280,128]{1,0:T(8,128)(2,1)S(1)} collective-permute-done((bf16[1280,128]{1,0:T(8,128)(2,1)S(1)}, bf16[1280,128]{1,0:T(8,128)(2,1)S(1)}, u32[]{:S(2)}, u32[]{:S(2)}) %collective-permute-start.3) | collective-permute-done | bytes 327712 | tf_op jit(solution)/shard_map/ppermute | solution.py:163
  80.4 0.0 collective-permute-done.2.row_other
  80.4 3.6 %shard_map.43 = bf16[2560,1280]{1,0:T(8,128)(2,1)} custom-call(s32[1]{0:T(128)} %bitcast.2.place_ref, bf16[2560,128]{1,0:T(8,128)(2,1)S(1)} %bitcast.24, bf16[2560,128]{1,0:T(8,128)(2,1)S(1)} %collective-permute-done.2.row_other, bf16[1280,128]{1,0:T(8,128)(2,1)S(1)} %get-tuple-element.19.col_mine, bf16[1280,128]{1,0:T(8,128)(2,1)S(1)} %collective-permute-done.3.col_other), custom_call_target="tpu_custom_call" | custom-call | flops 1677721600 | bytes 6553600 | tf_op jit(solution)/shard_map/pallas_call | solution.py:92
  (8 shorter events, 0.1 us)
Async XLA Ops:
  22.0 8.3 %collective-permute-start = (bf16[320,128]{1,0:T(8,128)(2,1)S(1)}, bf16[320,128]{1,0:T(8,128)(2,1)S(1)}, u32[]{:S(2)}, u32[]{:S(2)}) collective-permute-start(bf16[320,128]{1,0:T(8,128)(2,1)S(1)} %constant_dynamic-slice_fusion.2), channel_id=1, source_target_pairs={{0,64},{2,80},{4,32},{6,48},{8,0},{10,16},{12,96},{14,112},{16,66}... | collective-permute-start | bytes 245768 | tf_op jit(solution)/shard_map/ppermute | solution.py:143
  42.2 7.2 %collective-permute-start.1 = (bf16[320,128]{1,0:T(8,128)(2,1)S(1)}, bf16[320,128]{1,0:T(8,128)(2,1)S(1)}, u32[]{:S(2)}, u32[]{:S(2)}) collective-permute-start(bf16[320,128]{1,0:T(8,128)(2,1)S(1)} %get-tuple-element.21), channel_id=1, source_target_pairs={{64,0},{80,2},{32,4},{48,6},{0,8},{16,10},{96,12},{112,14},{66,16}... | collective-permute-start | bytes 245768 | tf_op jit(solution)/shard_map/ppermute | solution.py:152
  43.3 14.0 %all-to-all-start.2 = ((bf16[8,328,128]{2,1,0:T(8,128)(2,1)}), bf16[8,328,128]{2,1,0:T(8,128)(2,1)S(1)}, u32[]{:S(2)}, u32[]{:S(2)}) async-start(bf16[8,328,128]{2,1,0:T(8,128)(2,1)} %broadcast_in_dim.10), calls=%async_computation.2 | async-start | bytes 1343488 | tf_op jit(solution)/shard_map/all_to_all | solution.py:32
  71.3 9.0 %collective-permute-start.2 = (bf16[2560,128]{1,0:T(8,128)(2,1)S(1)}, bf16[2560,128]{1,0:T(8,128)(2,1)S(1)}, u32[]{:S(2)}, u32[]{:S(2)}) collective-permute-start(bf16[2560,128]{1,0:T(8,128)(2,1)S(1)} %bitcast.23), channel_id=1, source_target_pairs={{0,1},{1,0},{2,3},{3,2},{4,5},{5,4},{6,7},{7,6},{8,9},{9,8},{10,11... | collective-permute-start | bytes 1966088 | tf_op jit(solution)/shard_map/ppermute | solution.py:169
  78.3 2.1 %collective-permute-start.3 = (bf16[1280,128]{1,0:T(8,128)(2,1)S(1)}, bf16[1280,128]{1,0:T(8,128)(2,1)S(1)}, u32[]{:S(2)}, u32[]{:S(2)}) collective-permute-start(bf16[1280,128]{1,0:T(8,128)(2,1)S(1)} %get-tuple-element.18), channel_id=1, source_target_pairs={{0,1},{1,0},{2,3},{3,2},{4,5},{5,4},{6,7},{7,6},{8,9},{9,8},{10,11... | collective-permute-start | bytes 983048 | tf_op jit(solution)/shard_map/ppermute | solution.py:163

commit v6 on v5

--- a/solution.py
+++ b/solution.py
@@ -70,7 +70,7 @@
 def residual_kernel(place_ref, row_mine, row_other, col_mine, col_other, out_ref, turned, stage, sems):
     fields = row_mine.shape[1]
     tiles, tile, _ = stage.shape
-    turned[:fields, :] = col_mine[...].T
+    turned[:fields, :] = col_mine[...]
     turned[fields:, :] = col_other[...].T
     copies = []
     for at in range(tiles):
@@ -87,7 +87,7 @@
 
 def residual(place, row_mine, row_other, col_mine, col_other):
     pairs, fields = row_mine.shape
-    width = col_mine.shape[0]
+    width = col_mine.shape[1]
     tiles = 4
     return pl.pallas_call(
         residual_kernel,
@@ -168,7 +168,7 @@
     row_block = along[:, :width].reshape(-1, fields)
     rows_other = lax.ppermute(row_block, "depth", swap)
     place = row_index.reshape(1)
-    cycle_residual = residual(place, row_block, rows_other, cols_mine, cols_other)
+    cycle_residual = residual(place, row_block, rows_other, cols_mine.T, cols_other)
     return (cycle_residual, structure_factor)
 
 

time: 84.3 us -> 84.2 us (level)
  no operation moved by 1% of the time
where the time goes in v6:
time: 84.2 us; the launch traced here: 83.9 us
  blocking collectives  46 us (55%)
  starting transfers between devices  15.8 us (19%)
  waiting for transfers between devices  9.13 us (11%)
  Pallas kernels  9.1 us (11%)
  local copies, waits for them, and re-layouts  2.42 us (3%)
    all_to_all x2, blocking collectives, gather_blocks(): return lax.all_to_all(copies, axis, 0, 0)  34.2 us
    all_to_all x1, blocking collectives, body(): partial = lax.all_to_all(partial, 'row', 0, 0)  11.8 us
    all_to_all x1, waiting for transfers between devices, gather_blocks(): return lax.all_to_all(copies, axis, 0, 0)  7.86 us
    ppermute x1, starting transfers between devices, body(): rows_other = lax.ppermute(row_block, 'depth', swap)  6.84 us
    all_to_all x1, starting transfers between devices, gather_blocks(): return lax.all_to_all(copies, axis, 0, 0)  6.09 us
    pallas_call x1, Pallas kernels, dressing_part(): pl.pallas_call(functools.partial(dressing_kernel, bounds), in_specs=[VMEM...  5.54 us
    pallas_call x1, Pallas kernels, residual(): pl.pallas_call(residual_kernel, in_specs=[SMEM, VMEM, VMEM, VMEM, VMEM],...  3.55 us
    ppermute x1, starting transfers between devices, body(): vertex_here = lax.ppermute(piece, ('row', 'col'), pairs)  2.74 us
  transfers between devices with their start and end apart: 5, of which 2 were waited for; matrix products, arithmetic and copies ran while one was open for 2% of the time, Pallas kernels for 7%

profile of v6, /device:TPU:1, one launch (start us, length us, event | category | flops | bytes accessed | tf_op | source)
XLA Modules:
  0.0 83.9 jit_solution(15709960097621594826)
XLA Ops:
  0.6 1.0 %broadcast_in_dim.8 = bf16[8,320,128]{2,1,0:T(8,128)(2,1)S(1)} broadcast(bf16[320,128]{1,0:T(8,128)(2,1)} %bitcast.28), dimensions={1,2} | broadcast | bytes 737280 | tf_op jit(solution)/shard_map/broadcast_in_dim | solution.py:31
  1.6 20.4 %all_to_all.20 = bf16[8,320,128]{2,1,0:T(8,128)(2,1)S(1)} all-to-all(bf16[8,320,128]{2,1,0:T(8,128)(2,1)S(1)} %broadcast_in_dim.8), channel_id=1, replica_groups=mesh['row'=8,'col'=8,'depth'=2] {'col'}, dimensions={0} | all-to-all | bytes 1310720 | tf_op jit(solution)/shard_map/all_to_all | solution.py:32
  22.0 2.7 %collective-permute-start = (bf16[320,128]{1,0:T(8,128)(2,1)S(1)}, bf16[320,128]{1,0:T(8,128)(2,1)S(1)}, u32[]{:S(2)}, u32[]{:S(2)}) collective-permute-start(bf16[320,128]{1,0:T(8,128)(2,1)S(1)} %constant_dynamic-slice_fusion.1), channel_id=1, source_target_pairs={{0,64},{2,80},{4,32},{6,48},{8,0},{10,16},{12,96},{14,112},{16,66}... | collective-permute-start | bytes 245768 | tf_op jit(solution)/shard_map/ppermute | solution.py:143
  24.7 5.5 %shard_map.41 = bf16[2560,128]{1,0:T(8,128)(2,1)S(1)} custom-call(bf16[2560,128]{1,0:T(8,128)(2,1)S(1)} %bitcast.23, bf16[2560,2560]{1,0:T(8,128)(2,1)} %amplitudes_ref.1), custom_call_target="tpu_custom_call" | custom-call | flops 1677721600 | bytes 13107200 | tf_op jit(solution)/shard_map/pallas_call | solution.py:54
  30.3 0.0 collective-permute-done
  30.3 11.8 %all_to_all.21 = bf16[8,320,128]{2,1,0:T(8,128)(2,1)S(1)} all-to-all(bf16[8,320,128]{2,1,0:T(8,128)(2,1)S(1)} %bitcast.24), channel_id=1, replica_groups=mesh['row'=8,'col'=8,'depth'=2] {'row'}, dimensions={0} | all-to-all | bytes 1310720 | tf_op jit(solution)/shard_map/all_to_all | solution.py:146
  42.1 0.1 convert_reduce_fusion
  42.2 0.1 fusion.1
  42.2 0.1 collective-permute-start.1
  42.3 0.1 concatenate.6
  42.4 0.9 %broadcast_in_dim.10 = bf16[8,328,128]{2,1,0:T(8,128)(2,1)} broadcast(bf16[328,128]{1,0:T(8,128)(2,1)S(1)} %concatenate.6), dimensions={1,2} | broadcast | bytes 755712 | tf_op jit(solution)/shard_map/broadcast_in_dim | solution.py:31
  43.3 6.1 %all-to-all-start.2 = ((bf16[8,328,128]{2,1,0:T(8,128)(2,1)}), bf16[8,328,128]{2,1,0:T(8,128)(2,1)S(1)}, u32[]{:S(2)}, u32[]{:S(2)}) async-start(bf16[8,328,128]{2,1,0:T(8,128)(2,1)} %broadcast_in_dim.10), calls=%async_computation.2 | async-start | bytes 1343488 | tf_op jit(solution)/shard_map/all_to_all | solution.py:32
  49.4 7.9 %all-to-all-done.2 = bf16[8,328,128]{2,1,0:T(8,128)(2,1)S(1)} async-done(((bf16[8,328,128]{2,1,0:T(8,128)(2,1)}), bf16[8,328,128]{2,1,0:T(8,128)(2,1)S(1)}, u32[]{:S(2)}, u32[]{:S(2)}) %all-to-all-start.2) | async-done | bytes 671776 | tf_op jit(solution)/shard_map/all_to_all | solution.py:32
  57.3 0.1 concatenate.7
  57.4 0.1 broadcast_in_dim.11
  57.5 13.8 %all_to_all.22 = bf16[8,328,128]{2,1,0:T(8,128)(2,1)S(1)} all-to-all(bf16[8,328,128]{2,1,0:T(8,128)(2,1)S(1)} %broadcast_in_dim.11), channel_id=1, replica_groups=mesh['row'=8,'col'=8,'depth'=2] {'col'}, dimensions={0} | all-to-all | bytes 1343488 | tf_op jit(solution)/shard_map/all_to_all | solution.py:32
  71.3 6.8 %collective-permute-start.2 = (bf16[2560,128]{1,0:T(8,128)(2,1)S(1)}, bf16[2560,128]{1,0:T(8,128)(2,1)S(1)}, u32[]{:S(2)}, u32[]{:S(2)}) collective-permute-start(bf16[2560,128]{1,0:T(8,128)(2,1)S(1)} %bitcast.25), channel_id=1, source_target_pairs={{0,1},{1,0},{2,3},{3,2},{4,5},{5,4},{6,7},{7,6},{8,9},{9,8},{10,11... | collective-permute-start | bytes 1966088 | tf_op jit(solution)/shard_map/ppermute | solution.py:169
  78.2 0.1 constant_dynamic-slice_fusion
  78.3 0.1 collective-permute-start.3
  78.4 0.2 copy.4.col_mine
  78.6 0.5 convert_reduce_fusion.1
  79.1 1.3 %collective-permute-done.3.col_other = bf16[1280,128]{1,0:T(8,128)(2,1)S(1)} collective-permute-done((bf16[1280,128]{1,0:T(8,128)(2,1)S(1)}, bf16[1280,128]{1,0:T(8,128)(2,1)S(1)}, u32[]{:S(2)}, u32[]{:S(2)}) %collective-permute-start.3) | collective-permute-done | bytes 327712 | tf_op jit(solution)/shard_map/ppermute | solution.py:163
  80.4 0.0 collective-permute-done.2.row_other
  80.4 3.5 %shard_map.43 = bf16[2560,1280]{1,0:T(8,128)(2,1)} custom-call(s32[1]{0:T(128)} %bitcast.2.place_ref, bf16[2560,128]{1,0:T(8,128)(2,1)S(1)} %bitcast.26, bf16[2560,128]{1,0:T(8,128)(2,1)S(1)} %collective-permute-done.2.row_other, bf16[128,1280]{1,0:T(8,128)(2,1)S(1)} %copy.4.col_mine, bf16[1280,128]{1,0:T(8,128)(2,1)S(1)} %collective-permute-done.3.col_other), custom_call_target="tpu_custom_call" | custom-call | flops 1677721600 | bytes 6553600 | tf_op jit(solution)/shard_map/pallas_call | solution.py:92
  (9 shorter events, 0.2 us)
Async XLA Ops:
  22.0 8.3 %collective-permute-start = (bf16[320,128]{1,0:T(8,128)(2,1)S(1)}, bf16[320,128]{1,0:T(8,128)(2,1)S(1)}, u32[]{:S(2)}, u32[]{:S(2)}) collective-permute-start(bf16[320,128]{1,0:T(8,128)(2,1)S(1)} %constant_dynamic-slice_fusion.1), channel_id=1, source_target_pairs={{0,64},{2,80},{4,32},{6,48},{8,0},{10,16},{12,96},{14,112},{16,66}... | collective-permute-start | bytes 245768 | tf_op jit(solution)/shard_map/ppermute | solution.py:143
  42.2 7.2 %collective-permute-start.1 = (bf16[320,128]{1,0:T(8,128)(2,1)S(1)}, bf16[320,128]{1,0:T(8,128)(2,1)S(1)}, u32[]{:S(2)}, u32[]{:S(2)}) collective-permute-start(bf16[320,128]{1,0:T(8,128)(2,1)S(1)} %get-tuple-element.21), channel_id=1, source_target_pairs={{64,0},{80,2},{32,4},{48,6},{0,8},{16,10},{96,12},{112,14},{66,16}... | collective-permute-start | bytes 245768 | tf_op jit(solution)/shard_map/ppermute | solution.py:152
  43.3 14.0 %all-to-all-start.2 = ((bf16[8,328,128]{2,1,0:T(8,128)(2,1)}), bf16[8,328,128]{2,1,0:T(8,128)(2,1)S(1)}, u32[]{:S(2)}, u32[]{:S(2)}) async-start(bf16[8,328,128]{2,1,0:T(8,128)(2,1)} %broadcast_in_dim.10), calls=%async_computation.2 | async-start | bytes 1343488 | tf_op jit(solution)/shard_map/all_to_all | solution.py:32
  71.3 9.0 %collective-permute-start.2 = (bf16[2560,128]{1,0:T(8,128)(2,1)S(1)}, bf16[2560,128]{1,0:T(8,128)(2,1)S(1)}, u32[]{:S(2)}, u32[]{:S(2)}) collective-permute-start(bf16[2560,128]{1,0:T(8,128)(2,1)S(1)} %bitcast.25), channel_id=1, source_target_pairs={{0,1},{1,0},{2,3},{3,2},{4,5},{5,4},{6,7},{7,6},{8,9},{9,8},{10,11... | collective-permute-start | bytes 1966088 | tf_op jit(solution)/shard_map/ppermute | solution.py:169
  78.3 2.1 %collective-permute-start.3 = (bf16[1280,128]{1,0:T(8,128)(2,1)S(1)}, bf16[1280,128]{1,0:T(8,128)(2,1)S(1)}, u32[]{:S(2)}, u32[]{:S(2)}) collective-permute-start(bf16[1280,128]{1,0:T(8,128)(2,1)S(1)} %get-tuple-element.18), channel_id=1, source_target_pairs={{0,1},{1,0},{2,3},{3,2},{4,5},{5,4},{6,7},{7,6},{8,9},{9,8},{10,11... | collective-permute-start | bytes 983048 | tf_op jit(solution)/shard_map/ppermute | solution.py:163

commit v7 on v6

--- a/solution.py
+++ b/solution.py
@@ -24,7 +24,7 @@
 
 
 def served_pair(c, pair):
-    return ((c & ~1) + 2 - pair) & 3
+    return ((c >> 1) + 2 + (2 * (c & 1) - 1) * (pair - (c >> 1))) & 3
 
 
 def gather_blocks(block, axis):

time: 84.2 us -> 84.1 us (level)
    ppermute x1, starting transfers between devices: 6.84 us -> 5.07 us  [body(): rows_other = lax.ppermute(row_block, 'depth', swap)]
    all_to_all x1, starting transfers between devices: 6.09 us -> 7.19 us  [gather_blocks(): return lax.all_to_all(copies, axis, 0, 0)]
where the time goes in v7:
time: 84.1 us; the launch traced here: 83.7 us
  blocking collectives  46.4 us (55%)
  starting transfers between devices  15.2 us (18%)
  waiting for transfers between devices  9.18 us (11%)
  Pallas kernels  9.1 us (11%)
  local copies, waits for them, and re-layouts  2.42 us (3%)
    all_to_all x2, blocking collectives, gather_blocks(): return lax.all_to_all(copies, axis, 0, 0)  34.6 us
    all_to_all x1, blocking collectives, body(): partial = lax.all_to_all(partial, 'row', 0, 0)  11.8 us
    all_to_all x1, waiting for transfers between devices, gather_blocks(): return lax.all_to_all(copies, axis, 0, 0)  7.91 us
    all_to_all x1, starting transfers between devices, gather_blocks(): return lax.all_to_all(copies, axis, 0, 0)  7.19 us
    pallas_call x1, Pallas kernels, dressing_part(): pl.pallas_call(functools.partial(dressing_kernel, bounds), in_specs=[VMEM...  5.54 us
    ppermute x1, starting transfers between devices, body(): rows_other = lax.ppermute(row_block, 'depth', swap)  5.07 us
    pallas_call x1, Pallas kernels, residual(): pl.pallas_call(residual_kernel, in_specs=[SMEM, VMEM, VMEM, VMEM, VMEM],...  3.55 us
    ppermute x1, starting transfers between devices, body(): vertex_here = lax.ppermute(piece, ('row', 'col'), pairs)  2.74 us
  transfers between devices with their start and end apart: 5, of which 2 were waited for; matrix products, arithmetic and copies ran while one was open for 2% of the time, Pallas kernels for 7%

profile of v7, /device:TPU:1, one launch (start us, length us, event | category | flops | bytes accessed | tf_op | source)
XLA Modules:
  0.0 83.7 jit_solution(7389206823389330209)
XLA Ops:
  0.6 1.0 %broadcast_in_dim.8 = bf16[8,320,128]{2,1,0:T(8,128)(2,1)S(1)} broadcast(bf16[320,128]{1,0:T(8,128)(2,1)} %bitcast.28), dimensions={1,2} | broadcast | bytes 737280 | tf_op jit(solution)/shard_map/broadcast_in_dim | solution.py:31
  1.6 20.4 %all_to_all.20 = bf16[8,320,128]{2,1,0:T(8,128)(2,1)S(1)} all-to-all(bf16[8,320,128]{2,1,0:T(8,128)(2,1)S(1)} %broadcast_in_dim.8), channel_id=1, replica_groups=mesh['row'=8,'col'=8,'depth'=2] {'col'}, dimensions={0} | all-to-all | bytes 1310720 | tf_op jit(solution)/shard_map/all_to_all | solution.py:32
  22.0 2.7 %collective-permute-start = (bf16[320,128]{1,0:T(8,128)(2,1)S(1)}, bf16[320,128]{1,0:T(8,128)(2,1)S(1)}, u32[]{:S(2)}, u32[]{:S(2)}) collective-permute-start(bf16[320,128]{1,0:T(8,128)(2,1)S(1)} %constant_dynamic-slice_fusion.1), channel_id=1, source_target_pairs={{0,64},{2,80},{4,32},{6,48},{8,0},{10,16},{12,96},{14,112},{16,66}... | collective-permute-start | bytes 245768 | tf_op jit(solution)/shard_map/ppermute | solution.py:143
  24.7 5.5 %shard_map.41 = bf16[2560,128]{1,0:T(8,128)(2,1)S(1)} custom-call(bf16[2560,128]{1,0:T(8,128)(2,1)S(1)} %bitcast.23, bf16[2560,2560]{1,0:T(8,128)(2,1)} %amplitudes_ref.1), custom_call_target="tpu_custom_call" | custom-call | flops 1677721600 | bytes 13107200 | tf_op jit(solution)/shard_map/pallas_call | solution.py:54
  30.3 11.8 %all_to_all.21 = bf16[8,320,128]{2,1,0:T(8,128)(2,1)S(1)} all-to-all(bf16[8,320,128]{2,1,0:T(8,128)(2,1)S(1)} %bitcast.24), channel_id=1, replica_groups=mesh['row'=8,'col'=8,'depth'=2] {'row'}, dimensions={0} | all-to-all | bytes 1310720 | tf_op jit(solution)/shard_map/all_to_all | solution.py:146
  42.1 0.1 convert_reduce_fusion
  42.2 0.1 fusion.1
  42.2 0.1 collective-permute-start.1
  42.3 0.1 concatenate.6
  42.4 0.9 %broadcast_in_dim.10 = bf16[8,328,128]{2,1,0:T(8,128)(2,1)} broadcast(bf16[328,128]{1,0:T(8,128)(2,1)S(1)} %concatenate.6), dimensions={1,2} | broadcast | bytes 755712 | tf_op jit(solution)/shard_map/broadcast_in_dim | solution.py:31
  43.3 7.2 %all-to-all-start.2 = ((bf16[8,328,128]{2,1,0:T(8,128)(2,1)}), bf16[8,328,128]{2,1,0:T(8,128)(2,1)S(1)}, u32[]{:S(2)}, u32[]{:S(2)}) async-start(bf16[8,328,128]{2,1,0:T(8,128)(2,1)} %broadcast_in_dim.10), calls=%async_computation.2 | async-start | bytes 1343488 | tf_op jit(solution)/shard_map/all_to_all | solution.py:32
  50.5 0.0 collective-permute-done.1.block_ref
  50.5 7.9 %all-to-all-done.2 = bf16[8,328,128]{2,1,0:T(8,128)(2,1)S(1)} async-done(((bf16[8,328,128]{2,1,0:T(8,128)(2,1)}), bf16[8,328,128]{2,1,0:T(8,128)(2,1)S(1)}, u32[]{:S(2)}, u32[]{:S(2)}) %all-to-all-start.2) | async-done | bytes 671776 | tf_op jit(solution)/shard_map/all_to_all | solution.py:32
  58.5 0.1 concatenate.7
  58.5 0.1 broadcast_in_dim.11
  58.6 14.3 %all_to_all.22 = bf16[8,328,128]{2,1,0:T(8,128)(2,1)S(1)} all-to-all(bf16[8,328,128]{2,1,0:T(8,128)(2,1)S(1)} %broadcast_in_dim.11), channel_id=1, replica_groups=mesh['row'=8,'col'=8,'depth'=2] {'col'}, dimensions={0} | all-to-all | bytes 1343488 | tf_op jit(solution)/shard_map/all_to_all | solution.py:32
  72.9 5.1 %collective-permute-start.2 = (bf16[2560,128]{1,0:T(8,128)(2,1)S(1)}, bf16[2560,128]{1,0:T(8,128)(2,1)S(1)}, u32[]{:S(2)}, u32[]{:S(2)}) collective-permute-start(bf16[2560,128]{1,0:T(8,128)(2,1)S(1)} %bitcast.25), channel_id=1, source_target_pairs={{0,1},{1,0},{2,3},{3,2},{4,5},{5,4},{6,7},{7,6},{8,9},{9,8},{10,11... | collective-permute-start | bytes 1966088 | tf_op jit(solution)/shard_map/ppermute | solution.py:169
  78.0 0.1 constant_dynamic-slice_fusion
  78.1 0.1 collective-permute-start.3
  78.2 0.2 copy.4.col_mine
  78.4 0.5 convert_reduce_fusion.1
  78.9 1.3 %collective-permute-done.3.col_other = bf16[1280,128]{1,0:T(8,128)(2,1)S(1)} collective-permute-done((bf16[1280,128]{1,0:T(8,128)(2,1)S(1)}, bf16[1280,128]{1,0:T(8,128)(2,1)S(1)}, u32[]{:S(2)}, u32[]{:S(2)}) %collective-permute-start.3) | collective-permute-done | bytes 327712 | tf_op jit(solution)/shard_map/ppermute | solution.py:163
  80.2 0.0 collective-permute-done.2.row_other
  80.2 3.5 %shard_map.43 = bf16[2560,1280]{1,0:T(8,128)(2,1)} custom-call(s32[1]{0:T(128)} %bitcast.2.place_ref, bf16[2560,128]{1,0:T(8,128)(2,1)S(1)} %bitcast.26, bf16[2560,128]{1,0:T(8,128)(2,1)S(1)} %collective-permute-done.2.row_other, bf16[128,1280]{1,0:T(8,128)(2,1)S(1)} %copy.4.col_mine, bf16[1280,128]{1,0:T(8,128)(2,1)S(1)} %collective-permute-done.3.col_other), custom_call_target="tpu_custom_call" | custom-call | flops 1677721600 | bytes 6553600 | tf_op jit(solution)/shard_map/pallas_call | solution.py:92
  (9 shorter events, 0.2 us)
Async XLA Ops:
  22.0 8.3 %collective-permute-start = (bf16[320,128]{1,0:T(8,128)(2,1)S(1)}, bf16[320,128]{1,0:T(8,128)(2,1)S(1)}, u32[]{:S(2)}, u32[]{:S(2)}) collective-permute-start(bf16[320,128]{1,0:T(8,128)(2,1)S(1)} %constant_dynamic-slice_fusion.1), channel_id=1, source_target_pairs={{0,64},{2,80},{4,32},{6,48},{8,0},{10,16},{12,96},{14,112},{16,66}... | collective-permute-start | bytes 245768 | tf_op jit(solution)/shard_map/ppermute | solution.py:143
  42.2 8.3 %collective-permute-start.1 = (bf16[320,128]{1,0:T(8,128)(2,1)S(1)}, bf16[320,128]{1,0:T(8,128)(2,1)S(1)}, u32[]{:S(2)}, u32[]{:S(2)}) collective-permute-start(bf16[320,128]{1,0:T(8,128)(2,1)S(1)} %get-tuple-element.21), channel_id=1, source_target_pairs={{64,0},{80,2},{32,4},{48,6},{0,8},{16,10},{96,12},{112,14},{66,16}... | collective-permute-start | bytes 245768 | tf_op jit(solution)/shard_map/ppermute | solution.py:152
  43.3 15.1 %all-to-all-start.2 = ((bf16[8,328,128]{2,1,0:T(8,128)(2,1)}), bf16[8,328,128]{2,1,0:T(8,128)(2,1)S(1)}, u32[]{:S(2)}, u32[]{:S(2)}) async-start(bf16[8,328,128]{2,1,0:T(8,128)(2,1)} %broadcast_in_dim.10), calls=%async_computation.2 | async-start | bytes 1343488 | tf_op jit(solution)/shard_map/all_to_all | solution.py:32
  72.9 7.3 %collective-permute-start.2 = (bf16[2560,128]{1,0:T(8,128)(2,1)S(1)}, bf16[2560,128]{1,0:T(8,128)(2,1)S(1)}, u32[]{:S(2)}, u32[]{:S(2)}) collective-permute-start(bf16[2560,128]{1,0:T(8,128)(2,1)S(1)} %bitcast.25), channel_id=1, source_target_pairs={{0,1},{1,0},{2,3},{3,2},{4,5},{5,4},{6,7},{7,6},{8,9},{9,8},{10,11... | collective-permute-start | bytes 1966088 | tf_op jit(solution)/shard_map/ppermute | solution.py:169
  78.1 2.1 %collective-permute-start.3 = (bf16[1280,128]{1,0:T(8,128)(2,1)S(1)}, bf16[1280,128]{1,0:T(8,128)(2,1)S(1)}, u32[]{:S(2)}, u32[]{:S(2)}) collective-permute-start(bf16[1280,128]{1,0:T(8,128)(2,1)S(1)} %get-tuple-element.18), channel_id=1, source_target_pairs={{0,1},{1,0},{2,3},{3,2},{4,5},{5,4},{6,7},{7,6},{8,9},{9,8},{10,11... | collective-permute-start | bytes 983048 | tf_op jit(solution)/shard_map/ppermute | solution.py:163
